TPU v7x, 256 devices: a whole 4x4x8 slice. The times are simulated.
256 devices in a mesh: rows: 16 (over z_lo, x), tm: 16 (over y, z_hi, core).
Axes of the slice: x: 4, y: 4, z: 8 (z_hi: 2, z_lo: 4; z = z_hi * 4 + z_lo), core: 2. Of those that a mesh axis runs over, the one named last changes fastest.
Arguments:
- raw_signal: float32 [1024, 128, 128], P('tm', 'rows'), may hold values from -6 to 6
- fir_taps: float32 [61], replicated, may hold values from -0.75 to 0.75
- white_coef: float32 [25, 128, 128], P(None, 'rows'), may hold values from -1.25 to 1.25
- templates: bfloat16 [64, 61, 25], replicated, may hold values from -0.15625 to 0.15625
Outputs:
- whitened: bfloat16 [1024, 128, 128], P('tm', 'rows')
- best_score: float32 [1024, 128, 128], P('tm', 'rows')
All inputs are finite; a program needn't handle non-finite values.
Results may differ from a plain program's by a relative error of at most 0.0049.
Values may be sent and summed in bfloat16 or wider, within the bound.
No kernel may reach another device: no remote copies, remote signals or barrier semaphores. Data moves between devices by JAX's collectives and lax.ppermute only.
A program may use at most 64 MiB of HBM per device.

v0:
```python
import jax
import jax.numpy as jnp
from jax import lax
from jax.sharding import PartitionSpec as P


def shifted_2(array, axis, by):
    size = lax.axis_size(axis)
    pairs = [(i, i + by) for i in range(size) if 0 <= i + by < size]
    return lax.ppermute(array, axis, pairs)


def with_halo(block, sides, width):
    for axis, dim in sides:
        count = lax.axis_size(axis)
        forward = [(i, i + 1) for i in range(count - 1)]
        backward = [(target, source) for source, target in forward]
        low = lax.ppermute(
            lax.slice_in_dim(block, block.shape[dim] - width, None, axis=dim), axis, forward
        )
        high = lax.ppermute(lax.slice_in_dim(block, 0, width, axis=dim), axis, backward)
        block = jnp.concatenate([low, block, high], axis=dim)
    return block


def template_bands(templates, block_len):
    by_spot = jnp.transpose(templates, (0, 2, 1))
    tmpl_len = templates.shape[1]
    shifted = [jnp.pad(by_spot, ((0, 0), (0, 0), (b, block_len - 1 - b))) for b in range(block_len)]
    stacked = jnp.stack(shifted, axis=1)
    spot_major = stacked.reshape(templates.shape[0] * block_len, 25, tmpl_len + block_len - 1)
    return jnp.transpose(spot_major, (0, 2, 1)).reshape(
        templates.shape[0] * block_len, 25 * (tmpl_len + block_len - 1)
    )


def fir_band(fir_taps, num_rows):
    taps_back = fir_taps.shape[0] - 1
    span_len = num_rows + taps_back + 1
    tap_line = jnp.concatenate([fir_taps[::-1], jnp.zeros((num_rows,), jnp.float32)])
    tiled_line = jnp.tile(tap_line, num_rows)[: num_rows * (span_len - 1)]
    return tiled_line.reshape(num_rows, span_len - 1)


def filter_time(extended, fir_taps):
    taps_back = fir_taps.shape[0] - 1
    num_rows = extended.shape[0] - taps_back
    fir_matrix = fir_band(fir_taps, num_rows)
    flattened = extended.reshape(extended.shape[0], -1)
    product = jnp.dot(
        fir_matrix, flattened, precision=lax.Precision.HIGHEST, preferred_element_type=jnp.float32
    )
    return product.reshape(num_rows, extended.shape[1], extended.shape[2]).astype(jnp.bfloat16)


def whiten(rimmed, white_coef):
    row_count = white_coef.shape[1]
    col_count = white_coef.shape[2]
    padded = jnp.pad(rimmed, ((0, 0), (0, 0), (2, 2)))
    summed = jnp.zeros((rimmed.shape[0], row_count, col_count), jnp.float32)
    for row_off in range(5):
        for col_off in range(5):
            summed = summed + white_coef[5 * row_off + col_off] * padded[
                :, row_off : row_off + row_count, col_off : col_off + col_count
            ].astype(jnp.float32)
    return summed.astype(jnp.bfloat16)


def correlate(extended, band_matrix, num_templates, lag_len, step_count):
    block_len = 8
    row_count = extended.shape[1] - 4
    col_count = extended.shape[2]
    padded = jnp.pad(extended, ((0, 0), (0, 0), (2, 2)))
    span_len = padded.shape[0]
    spots = jnp.stack(
        [
            padded[:, row_off : row_off + row_count, col_off : col_off + col_count].reshape(
                span_len, row_count * col_count
            )
            for row_off in range(5)
            for col_off in range(5)
        ],
        axis=1,
    )

    def score_block(i):
        window = lax.dynamic_slice_in_dim(spots, i * block_len, block_len + lag_len, 0)
        flat_window = window.reshape((block_len + lag_len) * 25, row_count * col_count)
        scores = jnp.dot(band_matrix, flat_window, preferred_element_type=jnp.float32)
        return jnp.max(scores.reshape(num_templates, block_len, row_count * col_count), axis=0)

    best_rows = lax.map(score_block, jnp.arange(step_count // block_len, dtype=jnp.int32))
    return best_rows.reshape(step_count, row_count, col_count)


def shards(raw_signal, fir_taps, white_coef, templates):
    step_count = raw_signal.shape[0]
    taps_back = fir_taps.shape[0] - 1
    lag_len = templates.shape[1] - 1
    prev_part = shifted_2(raw_signal[step_count - taps_back :], "tm", 1)
    band_matrix = template_bands(templates, 8)
    filtered = filter_time(jnp.concatenate([prev_part, raw_signal]), fir_taps)
    rimmed = with_halo(filtered, (("rows", 1),), 2)
    whitened = whiten(rimmed, white_coef)
    widened = with_halo(whitened, (("rows", 1),), 2)
    next_part = shifted_2(widened[:lag_len], "tm", -1)
    extended = jnp.concatenate([widened, next_part])
    best_score = correlate(extended, band_matrix, templates.shape[0], lag_len, step_count)
    return (whitened, best_score)


def solution(mesh):
    return jax.shard_map(
        shards,
        mesh=mesh,
        in_specs=(P("tm", "rows", None), P(), P(None, "rows", None), P()),
        out_specs=(P("tm", "rows", None), P("tm", "rows", None)),
        check_vma=False,
    )
```

profile of v0, /device:TPU:14, one launch (start us, length us, event | category | flops | bytes accessed | tf_op | source)
XLA Modules:
  0.0 249.0 jit_solution(465197429874191690)
XLA Ops:
  16.0 3.7 %collective-permute-start.1 = (bf16[64,2,128]{2,0,1:T(8,128)(2,1)S(1)}, bf16[64,2,128]{2,0,1:T(8,128)(2,1)S(1)}, u32[]{:S(2)}, u32[]{:S(2)}) collective-permute-start(bf16[64,2,128]{2,0,1:T(8,128)(2,1)S(1)} %get-tuple-element.76), channel_id=1, source_target_pairs={{0,16},{16,32},{32,48},{48,64},{64,80},{80,96},{96,112},{112,128},... | collective-permute-start | bytes 98312 | tf_op jit(solution)/shard_map/ppermute | solution.py:18
  22.8 4.8 %collective-permute-done.2 = bf16[64,2,128]{2,0,1:T(8,128)(2,1)S(1)} collective-permute-done((bf16[64,2,128]{2,0,1:T(8,128)(2,1)S(1)}, bf16[64,2,128]{2,0,1:T(8,128)(2,1)S(1)}, u32[]{:S(2)}, u32[]{:S(2)}) %collective-permute-start.2) | collective-permute-done | bytes 32800 | tf_op jit(solution)/shard_map/ppermute | solution.py:21
  30.7 3.9 %collective-permute-start.4 = (bf16[64,2,128]{2,0,1:T(8,128)(2,1)S(1)}, bf16[64,2,128]{2,0,1:T(8,128)(2,1)S(1)}, u32[]{:S(2)}, u32[]{:S(2)}) collective-permute-start(bf16[64,2,128]{2,0,1:T(8,128)(2,1)S(1)} %get-tuple-element.75), channel_id=1, source_target_pairs={{16,0},{32,16},{48,32},{64,48},{80,64},{96,80},{112,96},{128,112},... | collective-permute-start | bytes 98312 | tf_op jit(solution)/shard_map/ppermute | solution.py:21
  39.3 5.7 %collective-permute-start.5 = (bf16[60,12,128]{2,0,1:T(8,128)(2,1)}, bf16[60,12,128]{2,0,1:T(8,128)(2,1)}, u32[]{:S(2)}, u32[]{:S(2)}) collective-permute-start(bf16[60,12,128]{2,0,1:T(8,128)(2,1)} %pad_maximum_fusion.2), channel_id=1, source_target_pairs={{1,0},{2,1},{3,2},{4,3},{5,4},{6,5},{7,6},{8,7},{9,8},{10,9},{11,1... | collective-permute-start | bytes 552968 | tf_op jit(solution)/shard_map/ppermute | solution.py:10
  46.9 4.9 %copy.42 = bf16[64,8,25,68]{3,1,0,2:T(8,128)(2,1)S(1)} copy(bf16[64,8,25,68]{3,0,2,1:T(8,128)(2,1)} %bitcast_dynamic-update-slice_fusion.1) | data formatting | bytes 3481600 | tf_op jit(solution)/shard_map/stack | solution.py:30
  51.8 4.7 %copy.35 = bf16[512,68,25]{0,2,1:T(8,128)(2,1)} copy(bf16[512,68,25]{1,0,2:T(8,128)(2,1)S(1)} %bitcast.188) | data formatting | bytes 3481600 | tf_op jit(solution)/shard_map/transpose | solution.py:32
  117.6 12.0 %copy.36 = bf16[124,25,1024]{2,1,0:T(8,128)(2,1)} copy(bf16[124,25,1024]{0,2,1:T(8,128)(2,1)} %bitcast_dynamic-update-slice_fusion.9) | data formatting | bytes 12697600 | tf_op jit(solution)/shard_map/while | solution.py:92
  129.6 117.7 %while.10 = (s32[]{:T(128)}, f32[8,8,1024]{2,1,0:T(8,128)}, s32[8]{0:T(128)S(1)}, bf16[124,25,1024]{2,1,0:T(8,128)(2,1)}, bf16[512,1700]{1,0:T(8,128)(2,1)}, /*index=5*/s32[]{:T(128)}, s32[1]{0:T(128)}, s32[]{:T(128)}, s32[]{:T(128)}) while((s32[]{:T(128)}, f32[8,8,1024]{2,1,0:T(8,128)}, s32[8]{0:T(128)S(1)}, ...), condition=%wide.region_2.3_spmd, body=%wide.region_0.2_spmd.sunk | while | flops 1783095296 | bytes 19247772 | solution.py:92
  130.9 5.2 %constant_dynamic-slice_fusion.2 = bf16[68,25,1024]{2,1,0:T(8,128)(2,1)} fusion(bf16[124,25,1024]{2,1,0:T(8,128)(2,1)} %get-tuple-element.155, s32[]{:T(128)S(6)} %select_n.4), kind=kLoop, calls=%fused_computation.2.clone.1 | loop fusion | bytes 6963204 | tf_op jit(solution)/shard_map/while/body/eval_jaxpr/dynamic_slice | solution.py:87
  136.0 4.1 %reshape.38 = bf16[1700,1024]{1,0:T(8,128)(2,1)S(1)} reshape(bf16[68,25,1024]{2,1,0:T(8,128)(2,1)} %constant_dynamic-slice_fusion.2) | data formatting | bytes 6963200 | tf_op jit(solution)/shard_map/while/body/eval_jaxpr/reshape | solution.py:88
  145.6 5.2 %constant_dynamic-slice_fusion.2 = bf16[68,25,1024]{2,1,0:T(8,128)(2,1)} fusion(bf16[124,25,1024]{2,1,0:T(8,128)(2,1)} %get-tuple-element.155, s32[]{:T(128)S(6)} %select_n.4), kind=kLoop, calls=%fused_computation.2.clone.1 | loop fusion | bytes 6963204 | tf_op jit(solution)/shard_map/while/body/eval_jaxpr/dynamic_slice | solution.py:87
  150.7 4.1 %reshape.38 = bf16[1700,1024]{1,0:T(8,128)(2,1)S(1)} reshape(bf16[68,25,1024]{2,1,0:T(8,128)(2,1)} %constant_dynamic-slice_fusion.2) | data formatting | bytes 6963200 | tf_op jit(solution)/shard_map/while/body/eval_jaxpr/reshape | solution.py:88
  160.3 5.2 %constant_dynamic-slice_fusion.2 = bf16[68,25,1024]{2,1,0:T(8,128)(2,1)} fusion(bf16[124,25,1024]{2,1,0:T(8,128)(2,1)} %get-tuple-element.155, s32[]{:T(128)S(6)} %select_n.4), kind=kLoop, calls=%fused_computation.2.clone.1 | loop fusion | bytes 6963204 | tf_op jit(solution)/shard_map/while/body/eval_jaxpr/dynamic_slice | solution.py:87
  165.4 4.1 %reshape.38 = bf16[1700,1024]{1,0:T(8,128)(2,1)S(1)} reshape(bf16[68,25,1024]{2,1,0:T(8,128)(2,1)} %constant_dynamic-slice_fusion.2) | data formatting | bytes 6963200 | tf_op jit(solution)/shard_map/while/body/eval_jaxpr/reshape | solution.py:88
  175.0 5.2 %constant_dynamic-slice_fusion.2 = bf16[68,25,1024]{2,1,0:T(8,128)(2,1)} fusion(bf16[124,25,1024]{2,1,0:T(8,128)(2,1)} %get-tuple-element.155, s32[]{:T(128)S(6)} %select_n.4), kind=kLoop, calls=%fused_computation.2.clone.1 | loop fusion | bytes 6963204 | tf_op jit(solution)/shard_map/while/body/eval_jaxpr/dynamic_slice | solution.py:87
  180.1 4.1 %reshape.38 = bf16[1700,1024]{1,0:T(8,128)(2,1)S(1)} reshape(bf16[68,25,1024]{2,1,0:T(8,128)(2,1)} %constant_dynamic-slice_fusion.2) | data formatting | bytes 6963200 | tf_op jit(solution)/shard_map/while/body/eval_jaxpr/reshape | solution.py:88
  189.7 5.2 %constant_dynamic-slice_fusion.2 = bf16[68,25,1024]{2,1,0:T(8,128)(2,1)} fusion(bf16[124,25,1024]{2,1,0:T(8,128)(2,1)} %get-tuple-element.155, s32[]{:T(128)S(6)} %select_n.4), kind=kLoop, calls=%fused_computation.2.clone.1 | loop fusion | bytes 6963204 | tf_op jit(solution)/shard_map/while/body/eval_jaxpr/dynamic_slice | solution.py:87
  194.8 4.1 %reshape.38 = bf16[1700,1024]{1,0:T(8,128)(2,1)S(1)} reshape(bf16[68,25,1024]{2,1,0:T(8,128)(2,1)} %constant_dynamic-slice_fusion.2) | data formatting | bytes 6963200 | tf_op jit(solution)/shard_map/while/body/eval_jaxpr/reshape | solution.py:88
  204.4 5.2 %constant_dynamic-slice_fusion.2 = bf16[68,25,1024]{2,1,0:T(8,128)(2,1)} fusion(bf16[124,25,1024]{2,1,0:T(8,128)(2,1)} %get-tuple-element.155, s32[]{:T(128)S(6)} %select_n.4), kind=kLoop, calls=%fused_computation.2.clone.1 | loop fusion | bytes 6963204 | tf_op jit(solution)/shard_map/while/body/eval_jaxpr/dynamic_slice | solution.py:87
  209.6 4.1 %reshape.38 = bf16[1700,1024]{1,0:T(8,128)(2,1)S(1)} reshape(bf16[68,25,1024]{2,1,0:T(8,128)(2,1)} %constant_dynamic-slice_fusion.2) | data formatting | bytes 6963200 | tf_op jit(solution)/shard_map/while/body/eval_jaxpr/reshape | solution.py:88
  219.1 5.2 %constant_dynamic-slice_fusion.2 = bf16[68,25,1024]{2,1,0:T(8,128)(2,1)} fusion(bf16[124,25,1024]{2,1,0:T(8,128)(2,1)} %get-tuple-element.155, s32[]{:T(128)S(6)} %select_n.4), kind=kLoop, calls=%fused_computation.2.clone.1 | loop fusion | bytes 6963204 | tf_op jit(solution)/shard_map/while/body/eval_jaxpr/dynamic_slice | solution.py:87
  224.3 4.1 %reshape.38 = bf16[1700,1024]{1,0:T(8,128)(2,1)S(1)} reshape(bf16[68,25,1024]{2,1,0:T(8,128)(2,1)} %constant_dynamic-slice_fusion.2) | data formatting | bytes 6963200 | tf_op jit(solution)/shard_map/while/body/eval_jaxpr/reshape | solution.py:88
  233.8 5.2 %constant_dynamic-slice_fusion.2 = bf16[68,25,1024]{2,1,0:T(8,128)(2,1)} fusion(bf16[124,25,1024]{2,1,0:T(8,128)(2,1)} %get-tuple-element.155, s32[]{:T(128)S(6)} %select_n.4), kind=kLoop, calls=%fused_computation.2.clone.1 | loop fusion | bytes 6963204 | tf_op jit(solution)/shard_map/while/body/eval_jaxpr/dynamic_slice | solution.py:87
  239.0 4.1 %reshape.38 = bf16[1700,1024]{1,0:T(8,128)(2,1)S(1)} reshape(bf16[68,25,1024]{2,1,0:T(8,128)(2,1)} %constant_dynamic-slice_fusion.2) | data formatting | bytes 6963200 | tf_op jit(solution)/shard_map/while/body/eval_jaxpr/reshape | solution.py:88
  (123 shorter events, 128.7 us)
Async XLA Ops:
  0.6 21.2 %copy-start = (bf16[64,61,25]{1,0,2:T(8,128)(2,1)S(1)}, bf16[64,61,25]{1,0,2:T(8,128)(2,1)}, u32[]{:S(2)}) copy-start(bf16[64,61,25]{1,0,2:T(8,128)(2,1)} %param.9) | copy-start | bytes 585604
  1.7 12.4 %collective-permute-start = (f32[60,8,128]{2,1,0:T(8,128)S(1)}, f32[60,8,128]{2,1,0:T(8,128)S(1)}, u32[]{:S(2)}, u32[]{:S(2)}) collective-permute-start(f32[60,8,128]{2,1,0:T(8,128)S(1)} %slice.260), channel_id=1, source_target_pairs={{0,1},{1,2},{2,3},{3,4},{4,5},{5,6},{6,7},{7,8},{8,9},{9,10},{10,1... | collective-permute-start | bytes 737288 | tf_op jit(solution)/shard_map/ppermute | solution.py:10
  16.0 6.8 %collective-permute-start.1 = (bf16[64,2,128]{2,0,1:T(8,128)(2,1)S(1)}, bf16[64,2,128]{2,0,1:T(8,128)(2,1)S(1)}, u32[]{:S(2)}, u32[]{:S(2)}) collective-permute-start(bf16[64,2,128]{2,0,1:T(8,128)(2,1)S(1)} %get-tuple-element.76), channel_id=1, source_target_pairs={{0,16},{16,32},{32,48},{48,64},{64,80},{80,96},{96,112},{112,128},... | collective-permute-start | bytes 98312 | tf_op jit(solution)/shard_map/ppermute | solution.py:18
  19.7 7.9 %collective-permute-start.2 = (bf16[64,2,128]{2,0,1:T(8,128)(2,1)S(1)}, bf16[64,2,128]{2,0,1:T(8,128)(2,1)S(1)}, u32[]{:S(2)}, u32[]{:S(2)}) collective-permute-start(bf16[64,2,128]{2,0,1:T(8,128)(2,1)S(1)} %get-tuple-element.77), channel_id=1, source_target_pairs={{16,0},{32,16},{48,32},{64,48},{80,64},{96,80},{112,96},{128,112},... | collective-permute-start | bytes 98312 | tf_op jit(solution)/shard_map/ppermute | solution.py:21
  28.7 6.8 %collective-permute-start.3 = (bf16[64,2,128]{2,0,1:T(8,128)(2,1)S(1)}, bf16[64,2,128]{2,0,1:T(8,128)(2,1)S(1)}, u32[]{:S(2)}, u32[]{:S(2)}) collective-permute-start(bf16[64,2,128]{2,0,1:T(8,128)(2,1)S(1)} %get-tuple-element.74), channel_id=1, source_target_pairs={{0,16},{16,32},{32,48},{48,64},{64,80},{80,96},{96,112},{112,128},... | collective-permute-start | bytes 98312 | tf_op jit(solution)/shard_map/ppermute | solution.py:18
  30.7 7.9 %collective-permute-start.4 = (bf16[64,2,128]{2,0,1:T(8,128)(2,1)S(1)}, bf16[64,2,128]{2,0,1:T(8,128)(2,1)S(1)}, u32[]{:S(2)}, u32[]{:S(2)}) collective-permute-start(bf16[64,2,128]{2,0,1:T(8,128)(2,1)S(1)} %get-tuple-element.75), channel_id=1, source_target_pairs={{16,0},{32,16},{48,32},{64,48},{80,64},{96,80},{112,96},{128,112},... | collective-permute-start | bytes 98312 | tf_op jit(solution)/shard_map/ppermute | solution.py:21
  39.3 23.1 %collective-permute-start.5 = (bf16[60,12,128]{2,0,1:T(8,128)(2,1)}, bf16[60,12,128]{2,0,1:T(8,128)(2,1)}, u32[]{:S(2)}, u32[]{:S(2)}) collective-permute-start(bf16[60,12,128]{2,0,1:T(8,128)(2,1)} %pad_maximum_fusion.2), channel_id=1, source_target_pairs={{1,0},{2,1},{3,2},{4,3},{5,4},{6,5},{7,6},{8,7},{9,8},{10,9},{11,1... | collective-permute-start | bytes 552968 | tf_op jit(solution)/shard_map/ppermute | solution.py:10
  67.1 18.3 %copy-start.3 = (bf16[124,8,128]{2,0,1:T(8,128)(2,1)S(1)}, bf16[124,8,128]{2,0,1:T(8,128)(2,1)}, u32[]{:S(2)}) copy-start(bf16[124,8,128]{2,0,1:T(8,128)(2,1)} %get-tuple-element.63) | copy-start | bytes 761860
  70.6 15.1 %copy-start.2 = (bf16[124,8,128]{2,0,1:T(8,128)(2,1)S(1)}, bf16[124,8,128]{2,0,1:T(8,128)(2,1)}, u32[]{:S(2)}) copy-start(bf16[124,8,128]{2,0,1:T(8,128)(2,1)} %get-tuple-element.64) | copy-start | bytes 761860
  78.8 8.2 %copy-start.1 = (bf16[124,8,128]{2,0,1:T(8,128)(2,1)S(1)}, bf16[124,8,128]{2,0,1:T(8,128)(2,1)}, u32[]{:S(2)}) copy-start(bf16[124,8,128]{2,0,1:T(8,128)(2,1)} %get-tuple-element.66) | copy-start | bytes 761860
where the time goes:
time: 252 us; the launch traced here: 249 us
  local copies, waits for them, and re-layouts  182 us (72%)
  matrix products  29.2 us (12%)
  starting transfers between devices  19.3 us (8%)
  waiting for transfers between devices  8.03 us (3%)
  loops' own time  5.39 us (2%)
  other arithmetic  3.69 us (1%)
    dynamic_slice x8, local copies, waits for them, and re-layouts, score_block(): lax.dynamic_slice_in_dim(spots, i * block_len, block_len + lag_len, 0)  41.3 us
    unnamed x41, local copies, waits for them, and re-layouts  40.9 us
    reshape x8, local copies, waits for them, and re-layouts, score_block(): window.reshape((block_len + lag_len) * 25, row_count * col_count)  32.8 us
    dot_general x8, matrix products, score_block(): jnp.dot(band_matrix, flat_window, preferred_element_type=jnp.float32)  28.5 us
    slice x27, local copies, waits for them, and re-layouts, correlate(): padded[:, row_off:row_off + row_count, col_off:col_off + col_count]  25.5 us
    while x2, local copies, waits for them, and re-layouts, correlate(): lax.map(score_block, jnp.arange(step_count // block_len, dtype=jnp.int32))  14.5 us
    ppermute x2, waiting for transfers between devices, with_halo(): lax.ppermute(lax.slice_in_dim(block, 0, width, axis=dim), axis, backward)  7.89 us
    ppermute x2, starting transfers between devices, shifted_2(): return lax.ppermute(array, axis, pairs)  7.66 us
  transfers between devices with their start and end apart: 6, of which 3 were waited for; matrix products, arithmetic and copies ran while one was open for 12% of the time, Pallas kernels for 0%

commit v1 on v0

v1 whole, which is shorter than its diff:
```python
import functools

import jax
import jax.numpy as jnp
from jax import lax
from jax.experimental import pallas as pl
from jax.experimental.pallas import tpu as pltpu
from jax.sharding import PartitionSpec as P

F32 = jnp.float32
BF16 = jnp.bfloat16
SHIFT = 4


def vmem():
    return pl.BlockSpec(memory_space=pltpu.VMEM)


def params():
    return pltpu.CompilerParams(vmem_limit_bytes=56 * 1024 * 1024)


def swap_pairs(array, axis, first):
    size = lax.axis_size(axis)
    pairs = []
    for low in range(first, size - 1, 2):
        pairs += [(low, low + 1), (low + 1, low)]
    return lax.ppermute(array, axis, pairs)


def step_by(array, axis, by):
    size = lax.axis_size(axis)
    return lax.ppermute(array, axis, [(i, i + by) for i in range(size) if 0 <= i + by < size])


def prep_kernel(line_ref, tmpl_ref, band_ref, lhs_ref, wide, mixed):
    spots, count, length = tmpl_ref.shape
    rows = band_ref.shape[0]
    line = jnp.broadcast_to(line_ref[...], (rows, 256))
    band = pltpu.roll(line, 0, 1, stride=1, stride_axis=0)
    high = band.astype(BF16)
    low = (band - high.astype(F32)).astype(BF16)
    band_ref[:, 0:256] = high
    band_ref[:, 256:512] = low
    band_ref[:, 512:768] = high

    wide[...] = jnp.zeros_like(wide)
    for s in range(spots):
        wide[s, :, 0:length] = tmpl_ref[s].astype(F32)
    for p in range((spots + 1) // 2):
        both = wide[2 * p]
        if 2 * p + 1 < spots:
            both = both + pltpu.roll(wide[2 * p + 1], 64, 1)
        for b in range(SHIFT):
            moved = pltpu.roll(both, b, 1) if b else both
            mixed[p, pl.ds(b, count, stride=SHIFT), :] = moved
        width = 128 if 2 * p + 1 < spots else 64
        lhs_ref[:, 128 * p : 128 * p + width] = mixed[p][:, :width].astype(BF16)


def prep(fir_taps, templates, span):
    count, length, spots = templates.shape
    taps = fir_taps.shape[0]
    line = jnp.pad(fir_taps[::-1], (span - taps + 1, 255 - span))[None]
    by_spot = jnp.transpose(templates, (2, 0, 1))
    return pl.pallas_call(
        prep_kernel,
        out_shape=(
            jax.ShapeDtypeStruct((2 * span, 768), BF16),
            jax.ShapeDtypeStruct((count * SHIFT, spots * 64), BF16),
        ),
        in_specs=[vmem()] * 2,
        out_specs=(vmem(), vmem()),
        scratch_shapes=[
            pltpu.VMEM((spots, count, 128), F32),
            pltpu.VMEM(((spots + 1) // 2, count * SHIFT, 128), F32),
        ],
        compiler_params=params(),
        cost_estimate=pl.CostEstimate(flops=10**7, bytes_accessed=2 * 10**6, transcendentals=0),
        name="prep",
    )(line, by_spot)


def fir_kernel(band_ref, raw_ref, near_ref, far_ref, coef_ref, filt_ref, up_ref, down_ref):
    rows, double, cols = filt_ref.shape
    span = double // 2
    even = lax.rem(lax.axis_index("tm"), 2) == 0
    columns = []
    for r in range(rows):
        near = near_ref[pl.ds(r, span, stride=rows), :]
        far = far_ref[pl.ds(r, span, stride=rows), :]
        own = raw_ref[pl.ds(r, span, stride=rows), :]
        before = jnp.where(even, far, near)
        after = jnp.where(even, near, far)
        line = jnp.concatenate([before, own, after, jnp.zeros_like(own)], axis=0)
        high = line.astype(BF16)
        low = (line - high.astype(F32)).astype(BF16)
        columns.append(jnp.concatenate([high, high, low], axis=0))
    for r in range(0, rows, 2):
        pair = jnp.concatenate(columns[r : r + 2], axis=1)
        out = jnp.dot(band_ref[...], pair, preferred_element_type=F32).astype(BF16)
        for k in range(2):
            piece = out[:, cols * k : cols * (k + 1)]
            filt_ref[r + k] = piece
            half = rows // 2
            side = up_ref if r + k < half else down_ref
            start = ((r + k) % half) * double
            side[start : start + double, :] = piece
    spots = coef_ref.shape[0] // rows
    base = rows // 2 * double
    for side, first in ((up_ref, 0), (down_ref, rows - 2)):
        side[base : base + 128, :] = jnp.zeros((128, cols), BF16)
        for k in range(2):
            coef = coef_ref[pl.ds(first + k, spots, stride=rows), :]
            high = coef.astype(BF16)
            low = (coef - high.astype(F32)).astype(BF16)
            side[base + 64 * k : base + 64 * k + spots, :] = high
            side[base + 64 * k + 32 : base + 64 * k + 32 + spots, :] = low


def fir(band, raw, near, far, coef, rows):
    span = raw.shape[0] // rows
    cols = raw.shape[1]
    message = jax.ShapeDtypeStruct((rows // 2 * 2 * span + 128, cols), BF16)
    return pl.pallas_call(
        fir_kernel,
        out_shape=(jax.ShapeDtypeStruct((rows, 2 * span, cols), BF16), message, message),
        in_specs=[vmem()] * 5,
        out_specs=(vmem(),) * 3,
        compiler_params=params(),
        cost_estimate=pl.CostEstimate(flops=2 * 10**8, bytes_accessed=2 * 10**6, transcendentals=0),
        name="fir",
    )(band, raw, near, far, coef)


def match_kernel(
    filt_ref, above_ref, below_ref, coef_ref, lhs_ref, white_ref, best_ref, moved, coefs, turn, slabs, natural, peaks
):
    rows, double, cols = filt_ref.shape
    span = double // 2
    half = rows // 2
    spots = coef_ref.shape[0] // rows
    wide = rows + 4
    lane = lax.broadcasted_iota(jnp.int32, (double, cols), 1)
    last = lax.axis_index("tm") == lax.axis_size("tm") - 1
    time = lax.broadcasted_iota(jnp.int32, (double, cols), 0)
    keep = jnp.logical_not(jnp.logical_and(last, time >= span))

    def shifted(x, b):
        if b == 2:
            return x
        out = pltpu.roll(x, (2 - b) % cols, 1)
        valid = lane >= 2 - b if b < 2 else lane < cols + 2 - b
        return jnp.where(valid, out, 0.0)

    def spread(x, row):
        x = x.astype(F32)
        for b in range(5):
            moved[b, row] = shifted(x, b)

    def from_above(k, _):
        spread(above_ref[pl.ds(pl.multiple_of(k * double, double), double), :], k)
        return 0

    def from_own(k, _):
        spread(filt_ref[k], half + k)
        return 0

    def from_below(k, _):
        spread(below_ref[pl.ds(pl.multiple_of(k * double, double), double), :], half + rows + k)
        return 0

    lax.fori_loop(0, half, from_above, 0)
    lax.fori_loop(0, rows, from_own, 0)
    lax.fori_loop(0, half, from_below, 0)

    base = half * double
    for k in range(2):
        for side, row in ((above_ref, k), (below_ref, rows + 2 + k)):
            high = side[base + 64 * k : base + 64 * k + 32, :].astype(F32)
            low = side[base + 64 * k + 32 : base + 64 * k + 64, :].astype(F32)
            coefs[row] = high + low
    for r in range(rows):
        coefs[2 + r, 0:spots] = coef_ref[pl.ds(r, spots, stride=rows), :]

    def whiten(r, _):
        total = jnp.zeros((double, cols), F32)
        for a in range(5):
            for b in range(5):
                s = 5 * a + b
                total = total + coefs[r, s : s + 1, :] * moved[b, r + half - 4 + a]
        total = jnp.where(keep, total, 0.0).astype(BF16).astype(F32)

        @pl.when(jnp.logical_and(r >= 2, r < rows + 2))
        def _():
            natural[pl.ds(r - 2, span, stride=rows), :] = total[:span]

        for b in range(5):
            turn[b, 0:double] = shifted(total, b)
            for f in range(4):
                slabs[f, b, r] = turn[b, SHIFT * f : SHIFT * f + double - 16, :].astype(BF16)
        return 0

    lax.fori_loop(0, wide, whiten, 0)
    white_ref[...] = natural[...].astype(BF16)

    def score(i, _):
        f = lax.rem(i, 4)
        start = pl.multiple_of(lax.div(i, 4) * 16, 16)
        for r in range(0, rows, 2):
            columns = [
                jnp.concatenate(
                    [slabs[f, b, r + k + a, pl.ds(start, 64), :] for a in range(5) for b in range(5)], axis=0
                )
                for k in range(2)
            ]
            window = jnp.concatenate(columns, axis=1)
            found = jnp.dot(lhs_ref[...], window, preferred_element_type=F32)
            top = jnp.max(found.reshape(found.shape[0] // 8, 8, 2 * cols), axis=0)
            top = jnp.maximum(top, pltpu.roll(top, 4, 0))
            peaks[i, r] = top[:, :cols]
            peaks[i, r + 1] = top[:, cols:]
        return 0

    steps = span // SHIFT
    lax.fori_loop(0, steps, score, 0)
    for i in range(steps):
        for r in range(rows):
            best_ref[pl.ds(SHIFT * rows * i + r, SHIFT, stride=rows), :] = peaks[i, r, 0:SHIFT, :]


def match(filt, above, below, coef, lhs):
    rows, double, cols = filt.shape
    span = double // 2
    return pl.pallas_call(
        match_kernel,
        out_shape=(
            jax.ShapeDtypeStruct((span * rows, cols), BF16),
            jax.ShapeDtypeStruct((span * rows, cols), F32),
        ),
        in_specs=[vmem()] * 5,
        out_specs=(vmem(), vmem()),
        scratch_shapes=[
            pltpu.VMEM((5, 2 * rows, double, cols), F32),
            pltpu.VMEM((rows + 4, 32, cols), F32),
            pltpu.VMEM((5, double, cols), F32),
            pltpu.VMEM((4, 5, rows + 4, double - 16, cols), BF16),
            pltpu.VMEM((span * rows, cols), F32),
            pltpu.VMEM((span // SHIFT, rows, 8, cols), F32),
        ],
        compiler_params=params(),
        cost_estimate=pl.CostEstimate(flops=14 * 10**9, bytes_accessed=2 * 10**6, transcendentals=0),
        name="match",
    )(filt, above, below, coef, lhs)


def shards(raw_signal, fir_taps, white_coef, templates):
    span, rows, cols = raw_signal.shape
    raw = raw_signal.reshape(span * rows, cols)
    coef = white_coef.reshape(-1, cols)
    far = swap_pairs(raw, "tm", 1)
    near = swap_pairs(raw, "tm", 0)
    band, lhs = prep(fir_taps, templates, span)
    filt, up, down = fir(band, raw, near, far, coef, rows)
    above = step_by(down, "rows", 1)
    below = step_by(up, "rows", -1)
    whitened, best = match(filt, above, below, coef, lhs)
    return whitened.reshape(span, rows, cols), best.reshape(span, rows, cols)


def solution(mesh):
    return jax.shard_map(
        shards,
        mesh=mesh,
        in_specs=(P("tm", "rows", None), P(), P(None, "rows", None), P()),
        out_specs=(P("tm", "rows", None), P("tm", "rows", None)),
        check_vma=False,
    )
```

time: 252 us -> 64.7 us (0.26); the launches traced: 249 us -> 64.5 us
  local copies, waits for them, and re-layouts: 182 us -> 2.19 us
  Pallas kernels: 0 us -> 30.7 us
  matrix products: 29.2 us -> 0 us
  waiting for transfers between devices: 8.03 us -> 15.6 us
  loops' own time: 5.39 us -> 0 us
  starting transfers between devices: 19.3 us -> 15.4 us
  other arithmetic: 3.69 us -> 0 us
    dynamic_slice x16 -> x0, local copies, waits for them, and re-layouts: 46 us -> none  [the longest x8 41.3 us: score_block(): lax.dynamic_slice_in_dim(spots, i * block_len, block_len + lag_len, 0)]
    unnamed x41 -> x10, local copies, waits for them, and re-layouts: 40.9 us -> 1.45 us
    reshape x11 -> x0, local copies, waits for them, and re-layouts: 35.8 us -> none  [the longest x8 32.8 us: score_block(): window.reshape((block_len + lag_len) * 25, row_count * col_count)]
    pallas_call x0 -> x3, Pallas kernels: none -> 30.7 us  [the longest x1 25 us: match(): pl.pallas_call(match_kernel, out_shape=(jax.ShapeDtypeStruct((span * rows...]
    dot_general x9 -> x0, matrix products: 29.2 us -> none  [the longest x8 28.5 us: score_block(): jnp.dot(band_matrix, flat_window, preferred_element_type=jnp.float32)]
    slice x30 -> x0, local copies, waits for them, and re-layouts: 26.5 us -> none  [the longest x27 25.5 us: correlate(): padded[:, row_off:row_off + row_count, col_off:col_off + col_count]]
    while x2 -> x0, local copies, waits for them, and re-layouts: 14.5 us -> none  [correlate(): lax.map(score_block, jnp.arange(step_count // block_len, dtype=jnp.int32))]
    ppermute x6 -> x4, waiting for transfers between devices: 8.03 us -> 15.6 us  [the longest x2 8.22 us: step_by(): lax.ppermute(array, axis, [(i, i + by) for i in range(size) if 0 <= i + b...]
  transfers between devices with their start and end apart: 6 -> 4, of which waited for: 3 -> 3; matrix products, arithmetic and copies ran while one was open for 12% -> 1% of each run, Pallas kernels for 0% -> 5%
where the time goes in v1:
time: 64.7 us; the launch traced here: 64.5 us
  Pallas kernels  30.7 us (47%)
  waiting for transfers between devices  15.6 us (24%)
  starting transfers between devices  15.4 us (24%)
  local copies, waits for them, and re-layouts  2.19 us (3%)
  between operations  0.67 us (1%)
    pallas_call x1, Pallas kernels, match(): pl.pallas_call(match_kernel, out_shape=(jax.ShapeDtypeStruct((span * rows...  25 us
    ppermute x2, starting transfers between devices, swap_pairs(): return lax.ppermute(array, axis, pairs)  9.3 us
    ppermute x2, waiting for transfers between devices, step_by(): lax.ppermute(array, axis, [(i, i + by) for i in range(size) if 0 <= i + b...  8.22 us
    ppermute x2, waiting for transfers between devices, swap_pairs(): return lax.ppermute(array, axis, pairs)  7.38 us
    ppermute x2, starting transfers between devices, step_by(): lax.ppermute(array, axis, [(i, i + by) for i in range(size) if 0 <= i + b...  6.08 us
    pallas_call x1, Pallas kernels, prep(): pl.pallas_call(prep_kernel, out_shape=(jax.ShapeDtypeStruct((2 * span, 76...  3.21 us
    pallas_call x1, Pallas kernels, fir(): pl.pallas_call(fir_kernel, out_shape=(jax.ShapeDtypeStruct((rows, 2 * spa...  2.44 us
    unnamed x10, local copies, waits for them, and re-layouts  1.45 us
  transfers between devices with their start and end apart: 4, of which 3 were waited for; matrix products, arithmetic and copies ran while one was open for 1% of the time, Pallas kernels for 5%

profile of v1, /device:TPU:14, one launch (start us, length us, event | category | flops | bytes accessed | tf_op | source)
XLA Modules:
  0.0 64.5 jit_solution(11959042771367079799)
XLA Ops:
  0.6 0.0 copy-start.4
  0.6 8.4 %collective-permute-start.1 = (f32[512,128]{1,0:T(8,128)}, f32[512,128]{1,0:T(8,128)S(1)}, u32[]{:S(2)}, u32[]{:S(2)}) collective-permute-start(f32[512,128]{1,0:T(8,128)} %bitcast.7), channel_id=1, source_target_pairs={{1,2},{2,1},{3,4},{4,3},{5,6},{6,5},{7,8},{8,7},{9,10},{10,9},{11,... | collective-permute-start | bytes 786440 | tf_op jit(solution)/shard_map/ppermute | solution.py:28
  9.1 0.9 %collective-permute-start = (f32[512,128]{1,0:T(8,128)}, f32[512,128]{1,0:T(8,128)S(1)}, u32[]{:S(2)}, u32[]{:S(2)}) collective-permute-start(f32[512,128]{1,0:T(8,128)} %bitcast.8), channel_id=1, source_target_pairs={{0,1},{1,0},{2,3},{3,2},{4,5},{5,4},{6,7},{7,6},{8,9},{9,8},{10,11... | collective-permute-start | bytes 786440 | tf_op jit(solution)/shard_map/ppermute | solution.py:28
  9.9 0.0 copy-done.4
  10.0 0.1 rev.3
  10.0 0.6 pad.4
  10.7 3.2 %prep.1 = (bf16[128,768]{1,0:T(8,128)(2,1)}, bf16[256,1600]{1,0:T(8,128)(2,1)}) custom-call(f32[1,256]{1,0:T(1,128)} %bitcast.12, bf16[25,64,61]{2,1,0:T(8,128)(2,1)} %bitcast.6), custom_call_target="tpu_custom_call" | custom-call | flops 10000000 | bytes 2000000 | tf_op jit(solution)/shard_map/prep/pallas_call | solution.py:66
  13.9 7.4 %collective-permute-done.1.far_ref = f32[512,128]{1,0:T(8,128)S(1)} collective-permute-done((f32[512,128]{1,0:T(8,128)}, f32[512,128]{1,0:T(8,128)S(1)}, u32[]{:S(2)}, u32[]{:S(2)}) %collective-permute-start.1) | collective-permute-done | bytes 262176 | tf_op jit(solution)/shard_map/ppermute | solution.py:28
  21.3 0.0 copy-start
  21.3 0.0 collective-permute-done.near_ref
  21.3 0.0 copy-start.1
  21.3 0.7 %copy-done = f32[512,128]{1,0:T(8,128)} copy-done((f32[512,128]{1,0:T(8,128)}, f32[512,128]{1,0:T(8,128)S(1)}, u32[]{:S(2)}) %copy-start) | copy-done | bytes 262168
  22.0 0.1 copy-done.1
  22.1 2.4 %fir.1 = (bf16[8,128,128]{2,1,0:T(8,128)(2,1)}, bf16[640,128]{1,0:T(8,128)(2,1)}, bf16[640,128]{1,0:T(8,128)(2,1)}) custom-call(bf16[128,768]{1,0:T(8,128)(2,1)} %get-tuple-element.9.band_ref, f32[512,128]{1,0:T(8,128)} %bitcast.9, f32[512,128]{1,0:T(8,128)} %copy-done.1, f32[512,128]{1,0:T(8,128)} %copy-done, f32[200,128]{1,0:T(8,128)} %bitcast.10), custom_call_target="tpu_custom_call" | custom-call | flops 200000000 | bytes 2000000 | tf_op jit(solution)/shard_map/fir/pallas_call | solution.py:125
  24.5 4.2 %collective-permute-start.2 = (bf16[640,128]{1,0:T(8,128)(2,1)}, bf16[640,128]{1,0:T(8,128)(2,1)S(1)}, u32[]{:S(2)}, u32[]{:S(2)}) collective-permute-start(bf16[640,128]{1,0:T(8,128)(2,1)} %get-tuple-element.11), channel_id=1, source_target_pairs={{0,16},{16,32},{32,48},{48,64},{64,80},{80,96},{96,112},{112,128},... | collective-permute-start | bytes 491528 | tf_op jit(solution)/shard_map/ppermute | solution.py:33
  28.7 1.9 %collective-permute-start.3 = (bf16[640,128]{1,0:T(8,128)(2,1)}, bf16[640,128]{1,0:T(8,128)(2,1)S(1)}, u32[]{:S(2)}, u32[]{:S(2)}) collective-permute-start(bf16[640,128]{1,0:T(8,128)(2,1)} %get-tuple-element.12), channel_id=1, source_target_pairs={{16,0},{32,16},{48,32},{64,48},{80,64},{96,80},{112,96},{128,112},... | collective-permute-start | bytes 491528 | tf_op jit(solution)/shard_map/ppermute | solution.py:33
  30.6 2.5 %collective-permute-done.2.above_ref = bf16[640,128]{1,0:T(8,128)(2,1)S(1)} collective-permute-done((bf16[640,128]{1,0:T(8,128)(2,1)}, bf16[640,128]{1,0:T(8,128)(2,1)S(1)}, u32[]{:S(2)}, u32[]{:S(2)}) %collective-permute-start.2) | collective-permute-done | bytes 163872 | tf_op jit(solution)/shard_map/ppermute | solution.py:33
  33.1 0.0 copy-start.2
  33.1 5.7 %collective-permute-done.3.below_ref = bf16[640,128]{1,0:T(8,128)(2,1)S(1)} collective-permute-done((bf16[640,128]{1,0:T(8,128)(2,1)}, bf16[640,128]{1,0:T(8,128)(2,1)S(1)}, u32[]{:S(2)}, u32[]{:S(2)}) %collective-permute-start.3) | collective-permute-done | bytes 163872 | tf_op jit(solution)/shard_map/ppermute | solution.py:33
  38.8 0.0 copy-start.3
  38.8 0.0 copy-done.2
  38.8 0.7 %copy-done.3 = bf16[640,128]{1,0:T(8,128)(2,1)} copy-done((bf16[640,128]{1,0:T(8,128)(2,1)}, bf16[640,128]{1,0:T(8,128)(2,1)S(1)}, u32[]{:S(2)}) %copy-start.3) | copy-done | bytes 163864
  39.5 25.0 %match.1 = (bf16[512,128]{1,0:T(8,128)(2,1)}, f32[512,128]{1,0:T(8,128)}) custom-call(bf16[8,128,128]{2,1,0:T(8,128)(2,1)} %get-tuple-element.10.filt_ref, bf16[640,128]{1,0:T(8,128)(2,1)} %copy-done.2, bf16[640,128]{1,0:T(8,128)(2,1)} %copy-done.3, f32[200,128]{1,0:T(8,128)} %bitcast.11, bf16[256,1600]{1,0:T(8,128)(2,1)} %get-tuple-element.13.lhs_ref), custom_call_target="tpu_custom_call" | custom-call | flops 14000000000 | bytes 2000000 | tf_op jit(solution)/shard_map/match/pallas_call | solution.py:235
Async XLA Ops:
  0.6 9.3 %copy-start.4 = (f32[61]{0:T(128)S(1)}, f32[61]{0:T(128)}, u32[]{:S(2)}) copy-start(f32[61]{0:T(128)} %param.5) | copy-start | bytes 736
  0.6 20.6 %collective-permute-start.1 = (f32[512,128]{1,0:T(8,128)}, f32[512,128]{1,0:T(8,128)S(1)}, u32[]{:S(2)}, u32[]{:S(2)}) collective-permute-start(f32[512,128]{1,0:T(8,128)} %bitcast.7), channel_id=1, source_target_pairs={{1,2},{2,1},{3,4},{4,3},{5,6},{6,5},{7,8},{8,7},{9,10},{10,9},{11,... | collective-permute-start | bytes 786440 | tf_op jit(solution)/shard_map/ppermute | solution.py:28
  9.1 12.2 %collective-permute-start = (f32[512,128]{1,0:T(8,128)}, f32[512,128]{1,0:T(8,128)S(1)}, u32[]{:S(2)}, u32[]{:S(2)}) collective-permute-start(f32[512,128]{1,0:T(8,128)} %bitcast.8), channel_id=1, source_target_pairs={{0,1},{1,0},{2,3},{3,2},{4,5},{5,4},{6,7},{7,6},{8,9},{9,8},{10,11... | collective-permute-start | bytes 786440 | tf_op jit(solution)/shard_map/ppermute | solution.py:28
  21.3 0.7 %copy-start = (f32[512,128]{1,0:T(8,128)}, f32[512,128]{1,0:T(8,128)S(1)}, u32[]{:S(2)}) copy-start(f32[512,128]{1,0:T(8,128)S(1)} %collective-permute-done.1.far_ref) | copy-start | bytes 786436
  21.3 0.8 %copy-start.1 = (f32[512,128]{1,0:T(8,128)}, f32[512,128]{1,0:T(8,128)S(1)}, u32[]{:S(2)}) copy-start(f32[512,128]{1,0:T(8,128)S(1)} %collective-permute-done.near_ref) | copy-start | bytes 786436
  24.5 8.6 %collective-permute-start.2 = (bf16[640,128]{1,0:T(8,128)(2,1)}, bf16[640,128]{1,0:T(8,128)(2,1)S(1)}, u32[]{:S(2)}, u32[]{:S(2)}) collective-permute-start(bf16[640,128]{1,0:T(8,128)(2,1)} %get-tuple-element.11), channel_id=1, source_target_pairs={{0,16},{16,32},{32,48},{48,64},{64,80},{80,96},{96,112},{112,128},... | collective-permute-start | bytes 491528 | tf_op jit(solution)/shard_map/ppermute | solution.py:33
  28.7 10.2 %collective-permute-start.3 = (bf16[640,128]{1,0:T(8,128)(2,1)}, bf16[640,128]{1,0:T(8,128)(2,1)S(1)}, u32[]{:S(2)}, u32[]{:S(2)}) collective-permute-start(bf16[640,128]{1,0:T(8,128)(2,1)} %get-tuple-element.12), channel_id=1, source_target_pairs={{16,0},{32,16},{48,32},{64,48},{80,64},{96,80},{112,96},{128,112},... | collective-permute-start | bytes 491528 | tf_op jit(solution)/shard_map/ppermute | solution.py:33
  33.1 5.7 %copy-start.2 = (bf16[640,128]{1,0:T(8,128)(2,1)}, bf16[640,128]{1,0:T(8,128)(2,1)S(1)}, u32[]{:S(2)}) copy-start(bf16[640,128]{1,0:T(8,128)(2,1)S(1)} %collective-permute-done.2.above_ref) | copy-start | bytes 491524
  38.8 0.7 %copy-start.3 = (bf16[640,128]{1,0:T(8,128)(2,1)}, bf16[640,128]{1,0:T(8,128)(2,1)S(1)}, u32[]{:S(2)}) copy-start(bf16[640,128]{1,0:T(8,128)(2,1)S(1)} %collective-permute-done.3.below_ref) | copy-start | bytes 491524

commit v2 on v1

--- a/solution.py
+++ b/solution.py
@@ -1,5 +1,3 @@
-import functools
-
 import jax
 import jax.numpy as jnp
 from jax import lax
@@ -7,6 +5,7 @@
 from jax.experimental.pallas import tpu as pltpu
 from jax.sharding import PartitionSpec as P
 
+
 F32 = jnp.float32
 BF16 = jnp.bfloat16
 SHIFT = 4
@@ -16,8 +15,8 @@
     return pl.BlockSpec(memory_space=pltpu.VMEM)
 
 
-def params():
-    return pltpu.CompilerParams(vmem_limit_bytes=56 * 1024 * 1024)
+def params(mib):
+    return pltpu.CompilerParams(vmem_limit_bytes=mib * 1024 * 1024)
 
 
 def swap_pairs(array, axis, first):
@@ -59,7 +58,7 @@
 
 
 def prep(fir_taps, templates, span):
-    count, length, spots = templates.shape
+    count, _, spots = templates.shape
     taps = fir_taps.shape[0]
     line = jnp.pad(fir_taps[::-1], (span - taps + 1, 255 - span))[None]
     by_spot = jnp.transpose(templates, (2, 0, 1))
@@ -75,20 +74,21 @@
             pltpu.VMEM((spots, count, 128), F32),
             pltpu.VMEM(((spots + 1) // 2, count * SHIFT, 128), F32),
         ],
-        compiler_params=params(),
+        compiler_params=params(8),
         cost_estimate=pl.CostEstimate(flops=10**7, bytes_accessed=2 * 10**6, transcendentals=0),
         name="prep",
     )(line, by_spot)
 
 
-def fir_kernel(band_ref, raw_ref, near_ref, far_ref, coef_ref, filt_ref, up_ref, down_ref):
+def fir_kernel(band_ref, raw_ref, near_ref, far_ref, coef_ref, filt_ref, up_ref, down_ref, widened):
     rows, double, cols = filt_ref.shape
     span = double // 2
     even = lax.rem(lax.axis_index("tm"), 2) == 0
+    widened[...] = far_ref[...].astype(F32)
     columns = []
     for r in range(rows):
         near = near_ref[pl.ds(r, span, stride=rows), :]
-        far = far_ref[pl.ds(r, span, stride=rows), :]
+        far = widened[pl.ds(r, span, stride=rows), :]
         own = raw_ref[pl.ds(r, span, stride=rows), :]
         before = jnp.where(even, far, near)
         after = jnp.where(even, near, far)
@@ -127,7 +127,8 @@
         out_shape=(jax.ShapeDtypeStruct((rows, 2 * span, cols), BF16), message, message),
         in_specs=[vmem()] * 5,
         out_specs=(vmem(),) * 3,
-        compiler_params=params(),
+        scratch_shapes=[pltpu.VMEM(raw.shape, F32)],
+        compiler_params=params(8),
         cost_estimate=pl.CostEstimate(flops=2 * 10**8, bytes_accessed=2 * 10**6, transcendentals=0),
         name="fir",
     )(band, raw, near, far, coef)
@@ -248,7 +249,7 @@
             pltpu.VMEM((span * rows, cols), F32),
             pltpu.VMEM((span // SHIFT, rows, 8, cols), F32),
         ],
-        compiler_params=params(),
+        compiler_params=params(20),
         cost_estimate=pl.CostEstimate(flops=14 * 10**9, bytes_accessed=2 * 10**6, transcendentals=0),
         name="match",
     )(filt, above, below, coef, lhs)
@@ -258,7 +259,7 @@
     span, rows, cols = raw_signal.shape
     raw = raw_signal.reshape(span * rows, cols)
     coef = white_coef.reshape(-1, cols)
-    far = swap_pairs(raw, "tm", 1)
+    far = swap_pairs(raw.astype(BF16), "tm", 1)
     near = swap_pairs(raw, "tm", 0)
     band, lhs = prep(fir_taps, templates, span)
     filt, up, down = fir(band, raw, near, far, coef, rows)

time: 64.7 us -> 54.8 us (0.85)
  waiting for transfers between devices: 15.6 us -> 9.5 us
  Pallas kernels: 30.7 us -> 25.3 us
  starting transfers between devices: 15.4 us -> 16.8 us
  local copies, waits for them, and re-layouts: 2.19 us -> 1.19 us
  other arithmetic: 0 us -> 0.97 us
    ppermute x2, waiting for transfers between devices: 7.38 us -> 1.49 us  [swap_pairs(): return lax.ppermute(array, axis, pairs)]
    pallas_call x1, Pallas kernels: 2.44 us -> 0.48 us  [fir(): pl.pallas_call(fir_kernel, out_shape=(jax.ShapeDtypeStruct((rows, 2 * spa...]
    pallas_call x1, Pallas kernels: 3.21 us -> 1.27 us  [prep(): pl.pallas_call(prep_kernel, out_shape=(jax.ShapeDtypeStruct((2 * span, 76...]
    pallas_call x1, Pallas kernels: 25 us -> 23.5 us  [match(): pl.pallas_call(match_kernel, out_shape=(jax.ShapeDtypeStruct((span * rows...]
    ppermute x2, starting transfers between devices: 6.08 us -> 7.5 us  [step_by(): lax.ppermute(array, axis, [(i, i + by) for i in range(size) if 0 <= i + b...]
    convert_element_type x0 -> x1, other arithmetic: none -> 0.97 us  [shards(): far = swap_pairs(raw.astype(BF16), 'tm', 1)]
    unnamed x10 -> x8, local copies, waits for them, and re-layouts: 1.45 us -> 1.02 us
  transfers between devices with their start and end apart: 4 -> 4, of which waited for: 3 -> 3; matrix products, arithmetic and copies ran while one was open for 1% -> 2% of each run, Pallas kernels for 5% -> 2%
where the time goes in v2:
time: 54.8 us; the launch traced here: 54.5 us
  Pallas kernels  25.3 us (46%)
  starting transfers between devices  16.8 us (31%)
  waiting for transfers between devices  9.5 us (17%)
  local copies, waits for them, and re-layouts  1.19 us (2%)
  other arithmetic  0.97 us (2%)
  between operations  0.71 us (1%)
    pallas_call x1, Pallas kernels, match(): pl.pallas_call(match_kernel, out_shape=(jax.ShapeDtypeStruct((span * rows...  23.5 us
    ppermute x2, starting transfers between devices, swap_pairs(): return lax.ppermute(array, axis, pairs)  9.31 us
    ppermute x2, waiting for transfers between devices, step_by(): lax.ppermute(array, axis, [(i, i + by) for i in range(size) if 0 <= i + b...  8.01 us
    ppermute x2, starting transfers between devices, step_by(): lax.ppermute(array, axis, [(i, i + by) for i in range(size) if 0 <= i + b...  7.5 us
    ppermute x2, waiting for transfers between devices, swap_pairs(): return lax.ppermute(array, axis, pairs)  1.49 us
    pallas_call x1, Pallas kernels, prep(): pl.pallas_call(prep_kernel, out_shape=(jax.ShapeDtypeStruct((2 * span, 76...  1.27 us
  transfers between devices with their start and end apart: 4, of which 3 were waited for; matrix products, arithmetic and copies ran while one was open for 2% of the time, Pallas kernels for 2%

profile of v2, /device:TPU:14, one launch (start us, length us, event | category | flops | bytes accessed | tf_op | source)
XLA Modules:
  0.0 54.5 jit_solution(254854904118045947)
XLA Ops:
  0.6 0.0 copy-start.3
  0.6 0.1 collective-permute-start
  0.7 1.0 %bitcast_convert_fusion = bf16[512,128]{1,0:T(8,128)(2,1)S(1)} fusion(f32[64,8,128]{2,1,0:T(8,128)} %param.4), kind=kLoop, calls=%fused_computation | loop fusion | flops 65536 | bytes 393216 | tf_op jit(solution)/shard_map/convert_element_type | solution.py:262
  1.7 0.0 copy-start
  1.7 9.2 %collective-permute-start.1 = (bf16[512,128]{1,0:T(8,128)(2,1)S(1)}, bf16[512,128]{1,0:T(8,128)(2,1)S(1)}, u32[]{:S(2)}, u32[]{:S(2)}) collective-permute-start(bf16[512,128]{1,0:T(8,128)(2,1)S(1)} %bitcast_convert_fusion), channel_id=1, source_target_pairs={{1,2},{2,1},{3,4},{4,3},{5,6},{6,5},{7,8},{8,7},{9,10},{10,9},{11,... | collective-permute-start | bytes 393224 | tf_op jit(solution)/shard_map/ppermute | solution.py:27
  10.9 0.0 copy-done.3
  11.0 0.1 rev.3
  11.1 0.1 pad.4
  11.1 0.0 copy-start.1
  11.1 1.0 %copy-done.1 = bf16[64,61,25]{1,0,2:T(8,128)(2,1)S(1)} copy-done((bf16[64,61,25]{1,0,2:T(8,128)(2,1)S(1)}, bf16[64,61,25]{1,0,2:T(8,128)(2,1)}, u32[]{:S(2)}) %copy-start.1) | copy-done | bytes 195224
  12.1 0.0 copy-start.2
  12.1 1.3 %prep.1 = (bf16[128,768]{1,0:T(8,128)(2,1)S(1)}, bf16[256,1600]{1,0:T(8,128)(2,1)S(1)}) custom-call(f32[1,256]{1,0:T(1,128)S(1)} %bitcast.12, bf16[25,64,61]{2,1,0:T(8,128)(2,1)S(1)} %bitcast.9), custom_call_target="tpu_custom_call" | custom-call | flops 10000000 | bytes 2000000 | tf_op jit(solution)/shard_map/prep/pallas_call | solution.py:65
  13.4 1.5 %collective-permute-done.1.far_ref = bf16[512,128]{1,0:T(8,128)(2,1)S(1)} collective-permute-done((bf16[512,128]{1,0:T(8,128)(2,1)S(1)}, bf16[512,128]{1,0:T(8,128)(2,1)S(1)}, u32[]{:S(2)}, u32[]{:S(2)}) %collective-permute-start.1) | collective-permute-done | bytes 131104 | tf_op jit(solution)/shard_map/ppermute | solution.py:27
  14.9 0.0 collective-permute-done.near_ref
  14.9 0.0 copy-done
  14.9 0.0 copy-done.2
  14.9 0.5 fir.1
  15.4 5.6 %collective-permute-start.2 = (bf16[640,128]{1,0:T(8,128)(2,1)S(1)}, bf16[640,128]{1,0:T(8,128)(2,1)S(1)}, u32[]{:S(2)}, u32[]{:S(2)}) collective-permute-start(bf16[640,128]{1,0:T(8,128)(2,1)S(1)} %get-tuple-element.11), channel_id=1, source_target_pairs={{0,16},{16,32},{32,48},{48,64},{64,80},{80,96},{96,112},{112,128},... | collective-permute-start | bytes 491528 | tf_op jit(solution)/shard_map/ppermute | solution.py:32
  21.0 1.9 %collective-permute-start.3 = (bf16[640,128]{1,0:T(8,128)(2,1)S(1)}, bf16[640,128]{1,0:T(8,128)(2,1)S(1)}, u32[]{:S(2)}, u32[]{:S(2)}) collective-permute-start(bf16[640,128]{1,0:T(8,128)(2,1)S(1)} %get-tuple-element.12), channel_id=1, source_target_pairs={{16,0},{32,16},{48,32},{64,48},{80,64},{96,80},{112,96},{128,112},... | collective-permute-start | bytes 491528 | tf_op jit(solution)/shard_map/ppermute | solution.py:32
  22.9 1.8 %collective-permute-done.2.above_ref = bf16[640,128]{1,0:T(8,128)(2,1)S(1)} collective-permute-done((bf16[640,128]{1,0:T(8,128)(2,1)S(1)}, bf16[640,128]{1,0:T(8,128)(2,1)S(1)}, u32[]{:S(2)}, u32[]{:S(2)}) %collective-permute-start.2) | collective-permute-done | bytes 163872 | tf_op jit(solution)/shard_map/ppermute | solution.py:32
  24.7 6.2 %collective-permute-done.3.below_ref = bf16[640,128]{1,0:T(8,128)(2,1)S(1)} collective-permute-done((bf16[640,128]{1,0:T(8,128)(2,1)S(1)}, bf16[640,128]{1,0:T(8,128)(2,1)S(1)}, u32[]{:S(2)}, u32[]{:S(2)}) %collective-permute-start.3) | collective-permute-done | bytes 163872 | tf_op jit(solution)/shard_map/ppermute | solution.py:32
  30.9 23.5 %match.1 = (bf16[512,128]{1,0:T(8,128)(2,1)}, f32[512,128]{1,0:T(8,128)}) custom-call(bf16[8,128,128]{2,1,0:T(8,128)(2,1)S(1)} %get-tuple-element.10.filt_ref, bf16[640,128]{1,0:T(8,128)(2,1)S(1)} %collective-permute-done.2.above_ref, bf16[640,128]{1,0:T(8,128)(2,1)S(1)} %collective-permute-done.3.below_ref, f32[200,128]{1,0:T(8,128)S(1)} %bitcast.11, ...), custom_call_target="tpu_custom_call" | custom-call | flops 14000000000 | bytes 2000000 | tf_op jit(solution)/shard_map/match/pallas_call | solution.py:236
Async XLA Ops:
  0.6 10.3 %copy-start.3 = (f32[61]{0:T(128)S(1)}, f32[61]{0:T(128)}, u32[]{:S(2)}) copy-start(f32[61]{0:T(128)} %param.5) | copy-start | bytes 736
  0.6 14.3 %collective-permute-start = (f32[512,128]{1,0:T(8,128)}, f32[512,128]{1,0:T(8,128)S(1)}, u32[]{:S(2)}, u32[]{:S(2)}) collective-permute-start(f32[512,128]{1,0:T(8,128)} %bitcast.7), channel_id=1, source_target_pairs={{0,1},{1,0},{2,3},{3,2},{4,5},{5,4},{6,7},{7,6},{8,9},{9,8},{10,11... | collective-permute-start | bytes 786440 | tf_op jit(solution)/shard_map/ppermute | solution.py:27
  1.7 13.2 %copy-start = (f32[64,8,128]{2,1,0:T(8,128)S(1)}, f32[64,8,128]{2,1,0:T(8,128)}, u32[]{:S(2)}) copy-start(f32[64,8,128]{2,1,0:T(8,128)} %param.4) | copy-start | bytes 786436
  1.7 13.2 %collective-permute-start.1 = (bf16[512,128]{1,0:T(8,128)(2,1)S(1)}, bf16[512,128]{1,0:T(8,128)(2,1)S(1)}, u32[]{:S(2)}, u32[]{:S(2)}) collective-permute-start(bf16[512,128]{1,0:T(8,128)(2,1)S(1)} %bitcast_convert_fusion), channel_id=1, source_target_pairs={{1,2},{2,1},{3,4},{4,3},{5,6},{6,5},{7,8},{8,7},{9,10},{10,9},{11,... | collective-permute-start | bytes 393224 | tf_op jit(solution)/shard_map/ppermute | solution.py:27
  11.1 1.0 %copy-start.1 = (bf16[64,61,25]{1,0,2:T(8,128)(2,1)S(1)}, bf16[64,61,25]{1,0,2:T(8,128)(2,1)}, u32[]{:S(2)}) copy-start(bf16[64,61,25]{1,0,2:T(8,128)(2,1)} %param.7) | copy-start | bytes 585604
  12.1 2.8 %copy-start.2 = (f32[25,8,128]{2,1,0:T(8,128)S(1)}, f32[25,8,128]{2,1,0:T(8,128)}, u32[]{:S(2)}) copy-start(f32[25,8,128]{2,1,0:T(8,128)} %param.6) | copy-start | bytes 307204
  15.4 9.3 %collective-permute-start.2 = (bf16[640,128]{1,0:T(8,128)(2,1)S(1)}, bf16[640,128]{1,0:T(8,128)(2,1)S(1)}, u32[]{:S(2)}, u32[]{:S(2)}) collective-permute-start(bf16[640,128]{1,0:T(8,128)(2,1)S(1)} %get-tuple-element.11), channel_id=1, source_target_pairs={{0,16},{16,32},{32,48},{48,64},{64,80},{80,96},{96,112},{112,128},... | collective-permute-start | bytes 491528 | tf_op jit(solution)/shard_map/ppermute | solution.py:32
  21.0 9.9 %collective-permute-start.3 = (bf16[640,128]{1,0:T(8,128)(2,1)S(1)}, bf16[640,128]{1,0:T(8,128)(2,1)S(1)}, u32[]{:S(2)}, u32[]{:S(2)}) collective-permute-start(bf16[640,128]{1,0:T(8,128)(2,1)S(1)} %get-tuple-element.12), channel_id=1, source_target_pairs={{16,0},{32,16},{48,32},{64,48},{80,64},{96,80},{112,96},{128,112},... | collective-permute-start | bytes 491528 | tf_op jit(solution)/shard_map/ppermute | solution.py:32

commit v3 on v2

v3 whole, which is shorter than its diff:
```python
import jax
import jax.numpy as jnp
from jax import lax
from jax.experimental import pallas as pl
from jax.experimental.pallas import tpu as pltpu
from jax.sharding import PartitionSpec as P


F32 = jnp.float32
BF16 = jnp.bfloat16
SHIFT = 4


def vmem():
    return pl.BlockSpec(memory_space=pltpu.VMEM)


def params(mib):
    return pltpu.CompilerParams(vmem_limit_bytes=mib * 1024 * 1024)


def swap_pairs(array, axis, first):
    size = lax.axis_size(axis)
    pairs = []
    for low in range(first, size - 1, 2):
        pairs += [(low, low + 1), (low + 1, low)]
    return lax.ppermute(array, axis, pairs)


def open_kernel(raw_ref, far_ref, keep_ref):
    skip = raw_ref.shape[0] - far_ref.shape[0]
    even = lax.rem(lax.axis_index("tm"), 2) == 0
    start = pl.multiple_of(jnp.where(even, 0, skip), 16)
    far_ref[...] = raw_ref[pl.ds(start, far_ref.shape[0]), :].astype(BF16)
    keep_ref[...] = raw_ref[...]


def opening(raw, rows, taps):
    return pl.pallas_call(
        open_kernel,
        out_shape=(
            jax.ShapeDtypeStruct(((taps - 1) * rows, raw.shape[1]), BF16),
            jax.ShapeDtypeStruct(raw.shape, F32),
        ),
        in_specs=[vmem()],
        out_specs=(vmem(), vmem()),
        compiler_params=params(4),
        cost_estimate=pl.CostEstimate(flops=10**5, bytes_accessed=10**6, transcendentals=0),
        name="opening",
    )(raw)


def prep_kernel(
    line_ref, tmpl_ref, coef_in_ref, band_ref, sum_ref, even_ref, odd_ref, coef_ref, wide, mixed
):
    coef_ref[...] = coef_in_ref[...]
    spots, count, length = tmpl_ref.shape
    rows = band_ref.shape[0]
    line = jnp.broadcast_to(line_ref[...], (rows, 256))
    band = pltpu.roll(line, 0, 1, stride=1, stride_axis=0)
    high = band.astype(BF16)
    low = (band - high.astype(F32)).astype(BF16)
    band_ref[:, 0:256] = high
    band_ref[:, 256:512] = low
    band_ref[:, 512:768] = high

    wide[...] = jnp.zeros_like(wide)
    for s in range(spots):
        wide[s, :, 0:length] = tmpl_ref[s].astype(F32)

    def even_spot(k):
        return wide[10 * (k // 5) + k % 5]

    def odd_spot(k):
        return wide[10 * (k // 5) + 5 + k % 5]

    def both_spots(k):
        return even_spot(k) + odd_spot(k) if k < 10 else even_spot(k)

    slot = 0
    for out_ref, piece, size in ((sum_ref, both_spots, 15), (even_ref, even_spot, 15), (odd_ref, odd_spot, 10)):
        for p in range(0, size, 2):
            pair = piece(p)
            if p + 1 < size:
                pair = pair + pltpu.roll(piece(p + 1), 64, 1)
            for b in range(SHIFT):
                moved = pltpu.roll(pair, b, 1) if b else pair
                mixed[slot, pl.ds(b, count, stride=SHIFT), :] = moved
            out_ref[:, 64 * p : 64 * p + 128] = mixed[slot].astype(BF16)
            slot += 1


def prep(fir_taps, templates, coef, span):
    count, _, spots = templates.shape
    taps = fir_taps.shape[0]
    line = jnp.pad(fir_taps[::-1], (span - taps + 1, 255 - span))[None]
    by_spot = jnp.transpose(templates, (2, 0, 1))
    return pl.pallas_call(
        prep_kernel,
        out_shape=(
            jax.ShapeDtypeStruct((2 * span, 768), BF16),
            jax.ShapeDtypeStruct((count * SHIFT, 16 * 64), BF16),
            jax.ShapeDtypeStruct((count * SHIFT, 16 * 64), BF16),
            jax.ShapeDtypeStruct((count * SHIFT, 10 * 64), BF16),
            jax.ShapeDtypeStruct(coef.shape, F32),
        ),
        in_specs=[vmem()] * 3,
        out_specs=(vmem(),) * 5,
        scratch_shapes=[
            pltpu.VMEM((spots, count, 128), F32),
            pltpu.VMEM((21, count * SHIFT, 128), F32),
        ],
        compiler_params=params(8),
        cost_estimate=pl.CostEstimate(flops=10**7, bytes_accessed=2 * 10**6, transcendentals=0),
        name="prep",
    )(line, by_spot, coef)


def fir_kernel(band_ref, raw_ref, near_ref, far_ref, coef_ref, filt_ref, first_ref, second_ref, widened):
    rows, double, cols = filt_ref.shape
    span = double // 2
    half = rows // 2
    even = lax.rem(lax.axis_index("tm"), 2) == 0
    short = far_ref.shape[0]
    skip = widened.shape[0] - short
    widened[0:skip, :] = jnp.zeros((skip, cols), F32)
    widened[short:, :] = jnp.zeros((skip, cols), F32)
    widened[pl.ds(pl.multiple_of(jnp.where(even, skip, 0), 16), short), :] = far_ref[...].astype(F32)
    columns = []
    for r in range(rows):
        near = near_ref[pl.ds(r, span, stride=rows), :]
        far = widened[pl.ds(r, span, stride=rows), :]
        own = raw_ref[pl.ds(r, span, stride=rows), :]
        before = jnp.where(even, far, near)
        after = jnp.where(even, near, far)
        line = jnp.concatenate([before, own, after, jnp.zeros_like(own)], axis=0)
        high = line.astype(BF16)
        low = (line - high.astype(F32)).astype(BF16)
        columns.append(jnp.concatenate([high, high, low], axis=0))
    for r in range(0, rows, 2):
        pair = jnp.concatenate(columns[r : r + 2], axis=1)
        out = jnp.dot(band_ref[...], pair, preferred_element_type=F32).astype(BF16)
        filt_ref[r] = out[:, :cols]
        filt_ref[r + 1] = out[:, cols:]
    spots = coef_ref.shape[0] // rows
    base = half * double
    upper = lax.rem(lax.axis_index("rows"), 2) == 0
    for side, at_end in ((first_ref, upper), (second_ref, jnp.logical_not(upper))):
        start = jnp.where(at_end, half, 0)
        for k in range(half):
            side[double * k : double * (k + 1), :] = filt_ref[start + k]
        side[base : base + 128, :] = jnp.zeros((128, cols), BF16)
        edge = jnp.where(at_end, rows - 2, 0)
        for k in range(2):
            coef = coef_ref[pl.ds(edge + k, spots, stride=rows), :]
            high = coef.astype(BF16)
            low = (coef - high.astype(F32)).astype(BF16)
            side[base + 64 * k : base + 64 * k + spots, :] = high
            side[base + 64 * k + 32 : base + 64 * k + 32 + spots, :] = low


def fir(band, raw, near, far, coef, rows):
    span = raw.shape[0] // rows
    cols = raw.shape[1]
    message = jax.ShapeDtypeStruct((rows // 2 * 2 * span + 128, cols), BF16)
    return pl.pallas_call(
        fir_kernel,
        out_shape=(jax.ShapeDtypeStruct((rows, 2 * span, cols), BF16), message, message),
        in_specs=[vmem()] * 5,
        out_specs=(vmem(),) * 3,
        scratch_shapes=[pltpu.VMEM(raw.shape, F32)],
        compiler_params=params(8),
        cost_estimate=pl.CostEstimate(flops=2 * 10**8, bytes_accessed=2 * 10**6, transcendentals=0),
        name="fir",
    )(band, raw, near, far, coef)


def shifter(shape):
    cols = shape[1]
    lane = lax.broadcasted_iota(jnp.int32, shape, 1)

    def shifted(x, b):
        if b == 2:
            return x
        out = pltpu.roll(x, (2 - b) % cols, 1)
        valid = lane >= 2 - b if b < 2 else lane < cols + 2 - b
        return jnp.where(valid, out, 0.0)

    return shifted


def closer(shape):
    span = shape[0] // 2
    last = lax.axis_index("tm") == lax.axis_size("tm") - 1
    time = lax.broadcasted_iota(jnp.int32, shape, 0)
    keep = jnp.logical_not(jnp.logical_and(last, time >= span))

    def closed(x):
        return jnp.where(keep, x, 0.0).astype(BF16).astype(F32)

    return closed


def build_slab(slab, x, turn, shifted):
    double = x.shape[0]
    for b in range(5):
        moved = shifted(x, b)
        turn[b] = moved
        for f in range(4):
            piece = moved[: double - 16] if f == 0 else turn[b, SHIFT * f : SHIFT * f + double - 16, :]
            slab[f, b] = piece.astype(BF16)


def inner_kernel(filt_ref, coef_ref, moved_ref, part_ref, white_ref, slab_ref, coefs, turn):
    rows, double, cols = filt_ref.shape
    spots = coef_ref.shape[0] // rows
    shifted = shifter((double, cols))
    closed = closer((double, cols))
    for r in range(rows):
        coefs[r, 0:spots] = coef_ref[pl.ds(r, spots, stride=rows), :]

    def spread(r, _):
        x = filt_ref[r].astype(F32)
        for b in range(5):
            moved_ref[b, r] = shifted(x, b)
        return 0

    lax.fori_loop(0, rows, spread, 0)

    def sums(r):
        total = jnp.zeros((double, cols), F32)
        for a in range(5):
            if 0 <= r + a - 2 < rows:
                for b in range(5):
                    s = 5 * a + b
                    total = total + coefs[r, s : s + 1, :] * moved_ref[b, r + a - 2]
        return total

    for k, r in enumerate((0, 1, rows - 2, rows - 1)):
        part_ref[k] = sums(r)
    for r in range(2, rows - 2):
        white_ref[r - 2] = closed(sums(r))
    build_slab(slab_ref.at[0], white_ref[1], turn, shifted)
    build_slab(slab_ref.at[1], white_ref[3], turn, shifted)
    build_slab(slab_ref.at[2], white_ref[0] - white_ref[1], turn, shifted)
    build_slab(slab_ref.at[3], white_ref[2] - white_ref[3], turn, shifted)
    build_slab(slab_ref.at[4], white_ref[2] - white_ref[1], turn, shifted)


def inner(filt, coef):
    rows, double, cols = filt.shape
    return pl.pallas_call(
        inner_kernel,
        out_shape=(
            jax.ShapeDtypeStruct((5, rows, double, cols), F32),
            jax.ShapeDtypeStruct((4, double, cols), F32),
            jax.ShapeDtypeStruct((rows - 4, double, cols), F32),
            jax.ShapeDtypeStruct((5, 4, 5, double - 16, cols), BF16),
        ),
        in_specs=[vmem()] * 2,
        out_specs=(vmem(),) * 4,
        scratch_shapes=[pltpu.VMEM((rows, 32, cols), F32), pltpu.VMEM((5, double, cols), F32)],
        compiler_params=params(12),
        cost_estimate=pl.CostEstimate(flops=10**9, bytes_accessed=10**7, transcendentals=0),
        name="inner",
    )(filt, coef)


def match_kernel(
    moved_ref,
    part_ref,
    mid_ref,
    mid_slab_ref,
    first_ref,
    second_ref,
    coef_ref,
    sum_ref,
    even_ref,
    odd_ref,
    white_ref,
    best_ref,
    halo,
    coefs,
    edge,
    white,
    turn,
    slabs,
    natural,
    peaks,
):
    rows, double, cols = moved_ref.shape[1:]
    span = double // 2
    half = rows // 2
    spots = coef_ref.shape[0] // rows
    base = half * double
    shifted = shifter((double, cols))
    closed = closer((double, cols))
    upper = lax.rem(lax.axis_index("rows"), 2) == 0

    for side, below in ((first_ref, upper), (second_ref, jnp.logical_not(upper))):
        dest = jnp.where(below, half, 0)

        def spread(k, _, side=side, dest=dest):
            x = side[pl.ds(pl.multiple_of(k * double, double), double), :].astype(F32)
            for b in range(5):
                halo[b, dest + k] = shifted(x, b)
            return 0

        lax.fori_loop(0, half, spread, 0)
        corner = jnp.where(below, 2, 0)
        for k in range(2):
            high = side[base + 64 * k : base + 64 * k + 32, :].astype(F32)
            low = side[base + 64 * k + 32 : base + 64 * k + 64, :].astype(F32)
            edge[corner + k] = high + low
    for k, r in enumerate((0, 1, rows - 2, rows - 1)):
        coefs[k, 0:spots] = coef_ref[pl.ds(r, spots, stride=rows), :]

    def line(b, row):
        if row < half:
            return halo[b, row]
        if row < half + rows:
            return moved_ref[b, row - half]
        return halo[b, row - rows]

    def outside(row):
        return row < half or row >= half + rows

    def sums(w):
        if w < 2 or w >= rows + 2:
            weights, total = edge.at[w if w < 2 else w - rows], jnp.zeros((double, cols), F32)
            offsets = range(5)
        else:
            k = w - 2 if w < 4 else w - rows + 2
            weights, total = coefs.at[k], part_ref[k]
            offsets = [a for a in range(5) if outside(w + a)]
        for a in offsets:
            for b in range(5):
                s = 5 * a + b
                total = total + weights[s : s + 1, :] * line(b, w + a)
        return closed(total)

    for w in (0, 1, 2, 3, rows, rows + 1, rows + 2, rows + 3):
        white[w] = sums(w)
    for w in range(4, rows):
        white[w] = mid_ref[w - 4]
    for r in range(rows):
        natural[pl.ds(r, span, stride=rows), :] = white[r + 2, 0:span]
    white_ref[...] = natural[...].astype(BF16)

    plain, level, step = {}, {}, {}
    plain[2], plain[3], level[2], level[3], step[2] = (mid_slab_ref.at[k] for k in range(5))
    spare = iter(range(12))
    for i in (0, 1, 4, 5):
        plain[i] = slabs.at[next(spare)]
        build_slab(plain[i], white[2 * i + 1], turn, shifted)
        level[i] = slabs.at[next(spare)]
        build_slab(level[i], white[2 * i] - white[2 * i + 1], turn, shifted)
    for i in (0, 1, 3, 4):
        step[i] = slabs.at[next(spare)]
        build_slab(step[i], white[2 * i + 2] - white[2 * i + 1], turn, shifted)

    def score(i, _):
        f = lax.rem(i, 4)
        start = pl.multiple_of(lax.div(i, 4) * 16, 16)

        def product(lhs_ref, source, m, depth):
            blank = [jnp.zeros((64, cols), BF16)] * (depth % 2)
            columns = [
                jnp.concatenate(
                    [source[m + k + j][f, b, pl.ds(start, 64), :] for j in range(depth) for b in range(5)] + blank,
                    axis=0,
                )
                for k in range(2)
            ]
            return jnp.dot(lhs_ref[...], jnp.concatenate(columns, axis=1), preferred_element_type=F32)

        def tiled(found):
            return found.reshape(found.shape[0] // 8, 8, 2 * cols)

        def top(found):
            high = jnp.max(found, axis=0)
            return jnp.maximum(high, pltpu.roll(high, 4, 0))

        for m in range(0, half, 2):
            shared = tiled(product(sum_ref, plain, m, 3))
            upper_row = top(tiled(product(even_ref, level, m, 3)) + shared)
            lower_row = top(tiled(product(odd_ref, step, m, 2)) + shared)
            for k in range(2):
                peaks[i, 2 * (m + k)] = upper_row[:, cols * k : cols * (k + 1)]
                peaks[i, 2 * (m + k) + 1] = lower_row[:, cols * k : cols * (k + 1)]
        return 0

    steps = span // SHIFT
    lax.fori_loop(0, steps, score, 0)
    for i in range(steps):
        for r in range(rows):
            best_ref[pl.ds(SHIFT * rows * i + r, SHIFT, stride=rows), :] = peaks[i, r, 0:SHIFT, :]


def match(inside, first, second, coef, bands):
    moved, part, mid, mid_slabs = inside
    rows, double, cols = moved.shape[1:]
    span = double // 2
    return pl.pallas_call(
        match_kernel,
        out_shape=(
            jax.ShapeDtypeStruct((span * rows, cols), BF16),
            jax.ShapeDtypeStruct((span * rows, cols), F32),
        ),
        in_specs=[vmem()] * 10,
        out_specs=(vmem(), vmem()),
        scratch_shapes=[
            pltpu.VMEM((5, rows, double, cols), F32),
            pltpu.VMEM((4, 32, cols), F32),
            pltpu.VMEM((4, 32, cols), F32),
            pltpu.VMEM((rows + 4, double, cols), F32),
            pltpu.VMEM((5, double, cols), F32),
            pltpu.VMEM((12, 4, 5, double - 16, cols), BF16),
            pltpu.VMEM((span * rows, cols), F32),
            pltpu.VMEM((span // SHIFT, rows, 8, cols), F32),
        ],
        compiler_params=params(24),
        cost_estimate=pl.CostEstimate(flops=11 * 10**9, bytes_accessed=10**7, transcendentals=0),
        name="match",
    )(moved, part, mid, mid_slabs, first, second, coef, *bands)


def shards(raw_signal, fir_taps, white_coef, templates):
    span, rows, cols = raw_signal.shape
    raw = raw_signal.reshape(span * rows, cols)
    coef = white_coef.reshape(-1, cols)
    far, raw = opening(raw, rows, fir_taps.shape[0])
    far = swap_pairs(far, "tm", 1)
    near = swap_pairs(raw, "tm", 0)
    band, *bands, coef = prep(fir_taps, templates, coef, span)
    filt, first, second = fir(band, raw, near, far, coef, rows)
    first = swap_pairs(first, "rows", 0)
    second = swap_pairs(second, "rows", 1)
    inside = inner(filt, coef)
    whitened, best = match(inside, first, second, coef, bands)
    return whitened.reshape(span, rows, cols), best.reshape(span, rows, cols)


def solution(mesh):
    return jax.shard_map(
        shards,
        mesh=mesh,
        in_specs=(P("tm", "rows", None), P(), P(None, "rows", None), P()),
        out_specs=(P("tm", "rows", None), P("tm", "rows", None)),
        check_vma=False,
    )
```

time: 54.8 us -> 47.4 us (0.86)
  the two profiles are of different devices: /device:TPU:14 before, /device:TPU:201 now
where the time goes in v3:
time: 47.4 us; the launch traced here: 47.1 us
  Pallas kernels  23.3 us (49%)
  waiting for transfers between devices  10.1 us (21%)
  starting transfers between devices  9.3 us (20%)
  local copies, waits for them, and re-layouts  3.66 us (8%)
  between operations  0.69 us (1%)
    pallas_call x1, Pallas kernels, match(): pl.pallas_call(match_kernel, out_shape=(jax.ShapeDtypeStruct((span * rows...  18.6 us
    ppermute x4, waiting for transfers between devices, swap_pairs(): return lax.ppermute(array, axis, pairs)  10.1 us
    ppermute x4, starting transfers between devices, swap_pairs(): return lax.ppermute(array, axis, pairs)  9.3 us
    unnamed x6, local copies, waits for them, and re-layouts  2.84 us
    pallas_call x1, Pallas kernels, inner(): pl.pallas_call(inner_kernel, out_shape=(jax.ShapeDtypeStruct((5, rows, do...  2.15 us
    pallas_call x1, Pallas kernels, prep(): pl.pallas_call(prep_kernel, out_shape=(jax.ShapeDtypeStruct((2 * span, 76...  2.04 us
  transfers between devices with their start and end apart: 4, of which 2 were waited for; matrix products, arithmetic and copies ran while one was open for 2% of the time, Pallas kernels for 9%

profile of v3, /device:TPU:201, one launch (start us, length us, event | category | flops | bytes accessed | tf_op | source)
XLA Modules:
  0.0 47.1 jit_solution(7040487771145778576)
XLA Ops:
  0.6 0.0 copy-start.1
  0.6 0.9 %copy-done.1 = f32[64,8,128]{2,1,0:T(8,128)S(1)} copy-done((f32[64,8,128]{2,1,0:T(8,128)S(1)}, f32[64,8,128]{2,1,0:T(8,128)}, u32[]{:S(2)}) %copy-start.1) | copy-done | bytes 262168
  1.6 0.8 %collective-permute-start = (f32[512,128]{1,0:T(8,128)S(1)}, f32[512,128]{1,0:T(8,128)S(1)}, u32[]{:S(2)}, u32[]{:S(2)}) collective-permute-start(f32[512,128]{1,0:T(8,128)S(1)} %get-tuple-element.19.raw_ref), channel_id=1, source_target_pairs={{0,1},{1,0},{2,3},{3,2},{4,5},{5,4},{6,7},{7,6},{8,9},{9,8},{10,11... | collective-permute-start | bytes 786440 | tf_op jit(solution)/shard_map/ppermute | solution.py:27
  2.4 3.1 %collective-permute-start.1 = (bf16[480,128]{1,0:T(8,128)(2,1)S(1)}, bf16[480,128]{1,0:T(8,128)(2,1)S(1)}, u32[]{:S(2)}, u32[]{:S(2)}) collective-permute-start(bf16[480,128]{1,0:T(8,128)(2,1)S(1)} %get-tuple-element.20), channel_id=1, source_target_pairs={{1,2},{2,1},{3,4},{4,3},{5,6},{6,5},{7,8},{8,7},{9,10},{10,9},{11,... | collective-permute-start | bytes 368648 | tf_op jit(solution)/shard_map/ppermute | solution.py:27
  5.5 0.7 %rev.3 = f32[61]{0:T(128)S(1)} reverse(f32[61]{0:T(128)} %param.5), dimensions={0} | reverse | bytes 488 | tf_op jit(solution)/shard_map/rev | solution.py:96
  6.2 0.1 pad.4
  6.3 0.0 copy-start
  6.3 1.0 %copy-done = bf16[64,61,25]{1,0,2:T(8,128)(2,1)S(1)} copy-done((bf16[64,61,25]{1,0,2:T(8,128)(2,1)S(1)}, bf16[64,61,25]{1,0,2:T(8,128)(2,1)}, u32[]{:S(2)}) %copy-start) | copy-done | bytes 195224
  7.3 0.0 copy-start.2
  7.3 0.9 %copy-done.2 = f32[25,8,128]{2,1,0:T(8,128)S(1)} copy-done((f32[25,8,128]{2,1,0:T(8,128)S(1)}, f32[25,8,128]{2,1,0:T(8,128)}, u32[]{:S(2)}) %copy-start.2) | copy-done | bytes 102424
  8.2 2.0 %prep.1 = (bf16[128,768]{1,0:T(8,128)(2,1)S(1)}, bf16[256,1024]{1,0:T(8,128)(2,1)S(1)}, bf16[256,1024]{1,0:T(8,128)(2,1)S(1)}, bf16[256,640]{1,0:T(8,128)(2,1)S(1)}, f32[200,128]{1,0:T(8,128)S(1)}) custom-call(f32[1,256]{1,0:T(1,128)S(1)} %bitcast.9, bf16[25,64,61]{2,1,0:T(8,128)(2,1)S(1)} %bitcast.6, f32[200,128]{1,0:T(8,128)S(1)} %bitcast.8), custom_call_target="tpu_custom_call" | custom-call | flops 10000000 | bytes 2000000 | tf_op jit(solution)/shard_map/prep/pallas_call | solution.py:98
  10.2 6.5 %collective-permute-done.1.far_ref = bf16[480,128]{1,0:T(8,128)(2,1)S(1)} collective-permute-done((bf16[480,128]{1,0:T(8,128)(2,1)S(1)}, bf16[480,128]{1,0:T(8,128)(2,1)S(1)}, u32[]{:S(2)}, u32[]{:S(2)}) %collective-permute-start.1) | collective-permute-done | bytes 122912 | tf_op jit(solution)/shard_map/ppermute | solution.py:27
  16.8 0.0 collective-permute-done.near_ref
  16.8 0.6 %fir.1 = (bf16[8,128,128]{2,1,0:T(8,128)(2,1)S(1)}, bf16[640,128]{1,0:T(8,128)(2,1)S(1)}, bf16[640,128]{1,0:T(8,128)(2,1)S(1)}) custom-call(bf16[128,768]{1,0:T(8,128)(2,1)S(1)} %get-tuple-element.18.band_ref, f32[512,128]{1,0:T(8,128)S(1)} %get-tuple-element.19.raw_ref, f32[512,128]{1,0:T(8,128)S(1)} %collective-permute-done.near_ref, ...), custom_call_target="tpu_custom_call" | custom-call | flops 200000000 | bytes 2000000 | tf_op jit(solution)/shard_map/fir/pallas_call | solution.py:166
  17.3 1.3 %collective-permute-start.2 = (bf16[640,128]{1,0:T(8,128)(2,1)S(1)}, bf16[640,128]{1,0:T(8,128)(2,1)S(1)}, u32[]{:S(2)}, u32[]{:S(2)}) collective-permute-start(bf16[640,128]{1,0:T(8,128)(2,1)S(1)} %get-tuple-element.27), channel_id=1, source_target_pairs={{0,16},{16,0},{32,48},{48,32},{64,80},{80,64},{96,112},{112,96},{1... | collective-permute-start | bytes 491528 | tf_op jit(solution)/shard_map/ppermute | solution.py:27
  18.6 4.2 %collective-permute-start.3 = (bf16[640,128]{1,0:T(8,128)(2,1)S(1)}, bf16[640,128]{1,0:T(8,128)(2,1)S(1)}, u32[]{:S(2)}, u32[]{:S(2)}) collective-permute-start(bf16[640,128]{1,0:T(8,128)(2,1)S(1)} %get-tuple-element.28), channel_id=1, source_target_pairs={{16,32},{32,16},{48,64},{64,48},{80,96},{96,80},{112,128},{128,112... | collective-permute-start | bytes 491528 | tf_op jit(solution)/shard_map/ppermute | solution.py:27
  22.8 2.2 %inner.1 = (f32[5,8,128,128]{3,2,1,0:T(8,128)S(1)}, f32[4,128,128]{2,1,0:T(8,128)S(1)}, f32[4,128,128]{2,1,0:T(8,128)S(1)}, bf16[5,4,5,112,128]{4,3,2,1,0:T(8,128)(2,1)S(1)}) custom-call(bf16[8,128,128]{2,1,0:T(8,128)(2,1)S(1)} %get-tuple-element.22.filt_ref, f32[200,128]{1,0:T(8,128)S(1)} %get-tuple-element.21.coef_ref), custom_call_target="tpu_custom_call" | custom-call | flops 1000000000 | bytes 10000000 | tf_op jit(solution)/shard_map/inner/pallas_call | solution.py:252
  25.0 0.0 collective-permute-done.2.first_ref
  25.0 3.6 %collective-permute-done.3.second_ref = bf16[640,128]{1,0:T(8,128)(2,1)S(1)} collective-permute-done((bf16[640,128]{1,0:T(8,128)(2,1)S(1)}, bf16[640,128]{1,0:T(8,128)(2,1)S(1)}, u32[]{:S(2)}, u32[]{:S(2)}) %collective-permute-start.3) | collective-permute-done | bytes 163872 | tf_op jit(solution)/shard_map/ppermute | solution.py:27
  28.6 18.6 %match.1 = (bf16[512,128]{1,0:T(8,128)(2,1)}, f32[512,128]{1,0:T(8,128)}) custom-call(f32[5,8,128,128]{3,2,1,0:T(8,128)S(1)} %get-tuple-element.23.moved_ref, f32[4,128,128]{2,1,0:T(8,128)S(1)} %get-tuple-element.24.part_ref, f32[4,128,128]{2,1,0:T(8,128)S(1)} %get-tuple-element.25.mid_ref, bf16[5,4,5,112,128]{4,3,2,1,0:T(8,128)(2,1)S(1)} %get-tuple-element.26.mid_slab_ref, ...), custom_call_target="tpu_custom_call" | custom-call | flops 11000000512 | bytes 10000000 | tf_op jit(solution)/shard_map/match/pallas_call | solution.py:404
  (1 shorter events, 0.0 us)
Async XLA Ops:
  0.6 1.0 %copy-start.1 = (f32[64,8,128]{2,1,0:T(8,128)S(1)}, f32[64,8,128]{2,1,0:T(8,128)}, u32[]{:S(2)}) copy-start(f32[64,8,128]{2,1,0:T(8,128)} %param.4) | copy-start | bytes 786436
  1.6 15.2 %collective-permute-start = (f32[512,128]{1,0:T(8,128)S(1)}, f32[512,128]{1,0:T(8,128)S(1)}, u32[]{:S(2)}, u32[]{:S(2)}) collective-permute-start(f32[512,128]{1,0:T(8,128)S(1)} %get-tuple-element.19.raw_ref), channel_id=1, source_target_pairs={{0,1},{1,0},{2,3},{3,2},{4,5},{5,4},{6,7},{7,6},{8,9},{9,8},{10,11... | collective-permute-start | bytes 786440 | tf_op jit(solution)/shard_map/ppermute | solution.py:27
  2.4 14.4 %collective-permute-start.1 = (bf16[480,128]{1,0:T(8,128)(2,1)S(1)}, bf16[480,128]{1,0:T(8,128)(2,1)S(1)}, u32[]{:S(2)}, u32[]{:S(2)}) collective-permute-start(bf16[480,128]{1,0:T(8,128)(2,1)S(1)} %get-tuple-element.20), channel_id=1, source_target_pairs={{1,2},{2,1},{3,4},{4,3},{5,6},{6,5},{7,8},{8,7},{9,10},{10,9},{11,... | collective-permute-start | bytes 368648 | tf_op jit(solution)/shard_map/ppermute | solution.py:27
  6.3 1.0 %copy-start = (bf16[64,61,25]{1,0,2:T(8,128)(2,1)S(1)}, bf16[64,61,25]{1,0,2:T(8,128)(2,1)}, u32[]{:S(2)}) copy-start(bf16[64,61,25]{1,0,2:T(8,128)(2,1)} %param.7) | copy-start | bytes 585604
  7.3 0.9 %copy-start.2 = (f32[25,8,128]{2,1,0:T(8,128)S(1)}, f32[25,8,128]{2,1,0:T(8,128)}, u32[]{:S(2)}) copy-start(f32[25,8,128]{2,1,0:T(8,128)} %param.6) | copy-start | bytes 307204
  17.3 7.6 %collective-permute-start.2 = (bf16[640,128]{1,0:T(8,128)(2,1)S(1)}, bf16[640,128]{1,0:T(8,128)(2,1)S(1)}, u32[]{:S(2)}, u32[]{:S(2)}) collective-permute-start(bf16[640,128]{1,0:T(8,128)(2,1)S(1)} %get-tuple-element.27), channel_id=1, source_target_pairs={{0,16},{16,0},{32,48},{48,32},{64,80},{80,64},{96,112},{112,96},{1... | collective-permute-start | bytes 491528 | tf_op jit(solution)/shard_map/ppermute | solution.py:27
  18.6 9.9 %collective-permute-start.3 = (bf16[640,128]{1,0:T(8,128)(2,1)S(1)}, bf16[640,128]{1,0:T(8,128)(2,1)S(1)}, u32[]{:S(2)}, u32[]{:S(2)}) collective-permute-start(bf16[640,128]{1,0:T(8,128)(2,1)S(1)} %get-tuple-element.28), channel_id=1, source_target_pairs={{16,32},{32,16},{48,64},{64,48},{80,96},{96,80},{112,128},{128,112... | collective-permute-start | bytes 491528 | tf_op jit(solution)/shard_map/ppermute | solution.py:27

commit v4 on v3

--- a/solution.py
+++ b/solution.py
@@ -277,8 +277,8 @@
     sum_ref,
     even_ref,
     odd_ref,
-    white_ref,
-    best_ref,
+    white_hbm,
+    best_hbm,
     halo,
     coefs,
     edge,
@@ -286,7 +286,9 @@
     turn,
     slabs,
     natural,
-    peaks,
+    rounded,
+    best,
+    sems,
 ):
     rows, double, cols = moved_ref.shape[1:]
     span = double // 2
@@ -345,7 +347,9 @@
         white[w] = mid_ref[w - 4]
     for r in range(rows):
         natural[pl.ds(r, span, stride=rows), :] = white[r + 2, 0:span]
-    white_ref[...] = natural[...].astype(BF16)
+    rounded[...] = natural[...].astype(BF16)
+    white_copy = pltpu.make_async_copy(rounded, white_hbm, sems.at[span // (4 * SHIFT)])
+    white_copy.start()
 
     plain, level, step = {}, {}, {}
     plain[2], plain[3], level[2], level[3], step[2] = (mid_slab_ref.at[k] for k in range(5))
@@ -359,42 +363,47 @@
         step[i] = slabs.at[next(spare)]
         build_slab(step[i], white[2 * i + 2] - white[2 * i + 1], turn, shifted)
 
-    def score(i, _):
-        f = lax.rem(i, 4)
-        start = pl.multiple_of(lax.div(i, 4) * 16, 16)
-
-        def product(lhs_ref, source, m, depth):
-            blank = [jnp.zeros((64, cols), BF16)] * (depth % 2)
-            columns = [
-                jnp.concatenate(
-                    [source[m + k + j][f, b, pl.ds(start, 64), :] for j in range(depth) for b in range(5)] + blank,
-                    axis=0,
-                )
-                for k in range(2)
-            ]
-            return jnp.dot(lhs_ref[...], jnp.concatenate(columns, axis=1), preferred_element_type=F32)
-
-        def tiled(found):
-            return found.reshape(found.shape[0] // 8, 8, 2 * cols)
-
-        def top(found):
-            high = jnp.max(found, axis=0)
-            return jnp.maximum(high, pltpu.roll(high, 4, 0))
-
-        for m in range(0, half, 2):
-            shared = tiled(product(sum_ref, plain, m, 3))
-            upper_row = top(tiled(product(even_ref, level, m, 3)) + shared)
-            lower_row = top(tiled(product(odd_ref, step, m, 2)) + shared)
-            for k in range(2):
-                peaks[i, 2 * (m + k)] = upper_row[:, cols * k : cols * (k + 1)]
-                peaks[i, 2 * (m + k) + 1] = lower_row[:, cols * k : cols * (k + 1)]
+    def product(lhs_ref, source, f, start, depth):
+        blank = [jnp.zeros((64, cols), BF16)] * (depth % 2)
+        columns = [
+            jnp.concatenate(
+                [source[m + j][f, b, pl.ds(start, 64), :] for j in range(depth) for b in range(5)] + blank, axis=0
+            )
+            for m in range(half)
+        ]
+        found = jnp.dot(lhs_ref[...], jnp.concatenate(columns, axis=1), preferred_element_type=F32)
+        return found.reshape(found.shape[0] // 8, 8, half * cols)
+
+    def top(found):
+        high = jnp.max(found, axis=0)
+        return jnp.maximum(high, pltpu.roll(high, 4, 0))
+
+    chunk = 4 * SHIFT * rows
+
+    def sent(q):
+        part = pl.ds(pl.multiple_of(q * chunk, chunk), chunk)
+        return pltpu.make_async_copy(best.at[part, :], best_hbm.at[part, :], sems.at[q])
+
+    def score(q, _):
+        start = pl.multiple_of(q * 16, 16)
+        for f in range(4):
+            shared = product(sum_ref, plain, f, start, 3)
+            found = (
+                top(product(even_ref, level, f, start, 3) + shared),
+                top(product(odd_ref, step, f, start, 2) + shared),
+            )
+            for r in range(rows):
+                first_row = q * chunk + SHIFT * rows * f + r
+                m = r // 2
+                best[pl.ds(first_row, SHIFT, stride=rows), :] = found[r % 2][0:SHIFT, cols * m : cols * (m + 1)]
+        sent(q).start()
         return 0
 
-    steps = span // SHIFT
-    lax.fori_loop(0, steps, score, 0)
-    for i in range(steps):
-        for r in range(rows):
-            best_ref[pl.ds(SHIFT * rows * i + r, SHIFT, stride=rows), :] = peaks[i, r, 0:SHIFT, :]
+    parts = span // (4 * SHIFT)
+    lax.fori_loop(0, parts, score, 0)
+    for q in range(parts):
+        sent(q).wait()
+    white_copy.wait()
 
 
 def match(inside, first, second, coef, bands):
@@ -408,7 +417,7 @@
             jax.ShapeDtypeStruct((span * rows, cols), F32),
         ),
         in_specs=[vmem()] * 10,
-        out_specs=(vmem(), vmem()),
+        out_specs=(pl.BlockSpec(memory_space=pltpu.HBM),) * 2,
         scratch_shapes=[
             pltpu.VMEM((5, rows, double, cols), F32),
             pltpu.VMEM((4, 32, cols), F32),
@@ -417,7 +426,9 @@
             pltpu.VMEM((5, double, cols), F32),
             pltpu.VMEM((12, 4, 5, double - 16, cols), BF16),
             pltpu.VMEM((span * rows, cols), F32),
-            pltpu.VMEM((span // SHIFT, rows, 8, cols), F32),
+            pltpu.VMEM((span * rows, cols), BF16),
+            pltpu.VMEM((span * rows, cols), F32),
+            pltpu.SemaphoreType.DMA((span // (4 * SHIFT) + 1,)),
         ],
         compiler_params=params(24),
         cost_estimate=pl.CostEstimate(flops=11 * 10**9, bytes_accessed=10**7, transcendentals=0),

time: 47.4 us -> 45.2 us (0.954)
  Pallas kernels: 23.3 us -> 21.1 us
    pallas_call x1, Pallas kernels: 18.6 us -> 16.4 us  [match(): pl.pallas_call(match_kernel, out_shape=(jax.ShapeDtypeStruct((span * rows...]
where the time goes in v4:
time: 45.2 us; the launch traced here: 44.9 us
  Pallas kernels  21.1 us (47%)
  waiting for transfers between devices  10.1 us (22%)
  starting transfers between devices  9.3 us (21%)
  local copies, waits for them, and re-layouts  3.66 us (8%)
  between operations  0.69 us (2%)
    pallas_call x1, Pallas kernels, match(): pl.pallas_call(match_kernel, out_shape=(jax.ShapeDtypeStruct((span * rows...  16.4 us
    ppermute x4, waiting for transfers between devices, swap_pairs(): return lax.ppermute(array, axis, pairs)  10.1 us
    ppermute x4, starting transfers between devices, swap_pairs(): return lax.ppermute(array, axis, pairs)  9.3 us
    unnamed x6, local copies, waits for them, and re-layouts  2.84 us
    pallas_call x1, Pallas kernels, inner(): pl.pallas_call(inner_kernel, out_shape=(jax.ShapeDtypeStruct((5, rows, do...  2.15 us
    pallas_call x1, Pallas kernels, prep(): pl.pallas_call(prep_kernel, out_shape=(jax.ShapeDtypeStruct((2 * span, 76...  2.04 us
  transfers between devices with their start and end apart: 4, of which 2 were waited for; matrix products, arithmetic and copies ran while one was open for 2% of the time, Pallas kernels for 9%

profile of v4, /device:TPU:201, one launch (start us, length us, event | category | flops | bytes accessed | tf_op | source)
XLA Modules:
  0.0 44.9 jit_solution(13332572459975073772)
XLA Ops:
  0.6 0.0 copy-start.1
  0.6 0.9 %copy-done.1 = f32[64,8,128]{2,1,0:T(8,128)S(1)} copy-done((f32[64,8,128]{2,1,0:T(8,128)S(1)}, f32[64,8,128]{2,1,0:T(8,128)}, u32[]{:S(2)}) %copy-start.1) | copy-done | bytes 262168
  1.6 0.8 %collective-permute-start = (f32[512,128]{1,0:T(8,128)S(1)}, f32[512,128]{1,0:T(8,128)S(1)}, u32[]{:S(2)}, u32[]{:S(2)}) collective-permute-start(f32[512,128]{1,0:T(8,128)S(1)} %get-tuple-element.19.raw_ref), channel_id=1, source_target_pairs={{0,1},{1,0},{2,3},{3,2},{4,5},{5,4},{6,7},{7,6},{8,9},{9,8},{10,11... | collective-permute-start | bytes 786440 | tf_op jit(solution)/shard_map/ppermute | solution.py:27
  2.4 3.1 %collective-permute-start.1 = (bf16[480,128]{1,0:T(8,128)(2,1)S(1)}, bf16[480,128]{1,0:T(8,128)(2,1)S(1)}, u32[]{:S(2)}, u32[]{:S(2)}) collective-permute-start(bf16[480,128]{1,0:T(8,128)(2,1)S(1)} %get-tuple-element.20), channel_id=1, source_target_pairs={{1,2},{2,1},{3,4},{4,3},{5,6},{6,5},{7,8},{8,7},{9,10},{10,9},{11,... | collective-permute-start | bytes 368648 | tf_op jit(solution)/shard_map/ppermute | solution.py:27
  5.5 0.7 %rev.3 = f32[61]{0:T(128)S(1)} reverse(f32[61]{0:T(128)} %param.5), dimensions={0} | reverse | bytes 488 | tf_op jit(solution)/shard_map/rev | solution.py:96
  6.2 0.1 pad.4
  6.3 0.0 copy-start
  6.3 1.0 %copy-done = bf16[64,61,25]{1,0,2:T(8,128)(2,1)S(1)} copy-done((bf16[64,61,25]{1,0,2:T(8,128)(2,1)S(1)}, bf16[64,61,25]{1,0,2:T(8,128)(2,1)}, u32[]{:S(2)}) %copy-start) | copy-done | bytes 195224
  7.3 0.0 copy-start.2
  7.3 0.9 %copy-done.2 = f32[25,8,128]{2,1,0:T(8,128)S(1)} copy-done((f32[25,8,128]{2,1,0:T(8,128)S(1)}, f32[25,8,128]{2,1,0:T(8,128)}, u32[]{:S(2)}) %copy-start.2) | copy-done | bytes 102424
  8.2 2.0 %prep.1 = (bf16[128,768]{1,0:T(8,128)(2,1)S(1)}, bf16[256,1024]{1,0:T(8,128)(2,1)S(1)}, bf16[256,1024]{1,0:T(8,128)(2,1)S(1)}, bf16[256,640]{1,0:T(8,128)(2,1)S(1)}, f32[200,128]{1,0:T(8,128)S(1)}) custom-call(f32[1,256]{1,0:T(1,128)S(1)} %bitcast.9, bf16[25,64,61]{2,1,0:T(8,128)(2,1)S(1)} %bitcast.6, f32[200,128]{1,0:T(8,128)S(1)} %bitcast.8), custom_call_target="tpu_custom_call" | custom-call | flops 10000000 | bytes 2000000 | tf_op jit(solution)/shard_map/prep/pallas_call | solution.py:98
  10.2 6.5 %collective-permute-done.1.far_ref = bf16[480,128]{1,0:T(8,128)(2,1)S(1)} collective-permute-done((bf16[480,128]{1,0:T(8,128)(2,1)S(1)}, bf16[480,128]{1,0:T(8,128)(2,1)S(1)}, u32[]{:S(2)}, u32[]{:S(2)}) %collective-permute-start.1) | collective-permute-done | bytes 122912 | tf_op jit(solution)/shard_map/ppermute | solution.py:27
  16.8 0.0 collective-permute-done.near_ref
  16.8 0.6 %fir.1 = (bf16[8,128,128]{2,1,0:T(8,128)(2,1)S(1)}, bf16[640,128]{1,0:T(8,128)(2,1)S(1)}, bf16[640,128]{1,0:T(8,128)(2,1)S(1)}) custom-call(bf16[128,768]{1,0:T(8,128)(2,1)S(1)} %get-tuple-element.18.band_ref, f32[512,128]{1,0:T(8,128)S(1)} %get-tuple-element.19.raw_ref, f32[512,128]{1,0:T(8,128)S(1)} %collective-permute-done.near_ref, ...), custom_call_target="tpu_custom_call" | custom-call | flops 200000000 | bytes 2000000 | tf_op jit(solution)/shard_map/fir/pallas_call | solution.py:166
  17.3 1.3 %collective-permute-start.2 = (bf16[640,128]{1,0:T(8,128)(2,1)S(1)}, bf16[640,128]{1,0:T(8,128)(2,1)S(1)}, u32[]{:S(2)}, u32[]{:S(2)}) collective-permute-start(bf16[640,128]{1,0:T(8,128)(2,1)S(1)} %get-tuple-element.27), channel_id=1, source_target_pairs={{0,16},{16,0},{32,48},{48,32},{64,80},{80,64},{96,112},{112,96},{1... | collective-permute-start | bytes 491528 | tf_op jit(solution)/shard_map/ppermute | solution.py:27
  18.6 4.2 %collective-permute-start.3 = (bf16[640,128]{1,0:T(8,128)(2,1)S(1)}, bf16[640,128]{1,0:T(8,128)(2,1)S(1)}, u32[]{:S(2)}, u32[]{:S(2)}) collective-permute-start(bf16[640,128]{1,0:T(8,128)(2,1)S(1)} %get-tuple-element.28), channel_id=1, source_target_pairs={{16,32},{32,16},{48,64},{64,48},{80,96},{96,80},{112,128},{128,112... | collective-permute-start | bytes 491528 | tf_op jit(solution)/shard_map/ppermute | solution.py:27
  22.8 2.2 %inner.1 = (f32[5,8,128,128]{3,2,1,0:T(8,128)S(1)}, f32[4,128,128]{2,1,0:T(8,128)S(1)}, f32[4,128,128]{2,1,0:T(8,128)S(1)}, bf16[5,4,5,112,128]{4,3,2,1,0:T(8,128)(2,1)S(1)}) custom-call(bf16[8,128,128]{2,1,0:T(8,128)(2,1)S(1)} %get-tuple-element.22.filt_ref, f32[200,128]{1,0:T(8,128)S(1)} %get-tuple-element.21.coef_ref), custom_call_target="tpu_custom_call" | custom-call | flops 1000000000 | bytes 10000000 | tf_op jit(solution)/shard_map/inner/pallas_call | solution.py:252
  25.0 0.0 collective-permute-done.2.first_ref
  25.0 3.6 %collective-permute-done.3.second_ref = bf16[640,128]{1,0:T(8,128)(2,1)S(1)} collective-permute-done((bf16[640,128]{1,0:T(8,128)(2,1)S(1)}, bf16[640,128]{1,0:T(8,128)(2,1)S(1)}, u32[]{:S(2)}, u32[]{:S(2)}) %collective-permute-start.3) | collective-permute-done | bytes 163872 | tf_op jit(solution)/shard_map/ppermute | solution.py:27
  28.6 16.4 %match.1 = (bf16[512,128]{1,0:T(8,128)(2,1)}, f32[512,128]{1,0:T(8,128)}) custom-call(f32[5,8,128,128]{3,2,1,0:T(8,128)S(1)} %get-tuple-element.23.moved_ref, f32[4,128,128]{2,1,0:T(8,128)S(1)} %get-tuple-element.24.part_ref, f32[4,128,128]{2,1,0:T(8,128)S(1)} %get-tuple-element.25.mid_ref, bf16[5,4,5,112,128]{4,3,2,1,0:T(8,128)(2,1)S(1)} %get-tuple-element.26.mid_slab_ref, ...), custom_call_target="tpu_custom_call" | custom-call | flops 11000000512 | bytes 10000000 | tf_op jit(solution)/shard_map/match/pallas_call | solution.py:413
  (1 shorter events, 0.0 us)
Async XLA Ops:
  0.6 1.0 %copy-start.1 = (f32[64,8,128]{2,1,0:T(8,128)S(1)}, f32[64,8,128]{2,1,0:T(8,128)}, u32[]{:S(2)}) copy-start(f32[64,8,128]{2,1,0:T(8,128)} %param.4) | copy-start | bytes 786436
  1.6 15.2 %collective-permute-start = (f32[512,128]{1,0:T(8,128)S(1)}, f32[512,128]{1,0:T(8,128)S(1)}, u32[]{:S(2)}, u32[]{:S(2)}) collective-permute-start(f32[512,128]{1,0:T(8,128)S(1)} %get-tuple-element.19.raw_ref), channel_id=1, source_target_pairs={{0,1},{1,0},{2,3},{3,2},{4,5},{5,4},{6,7},{7,6},{8,9},{9,8},{10,11... | collective-permute-start | bytes 786440 | tf_op jit(solution)/shard_map/ppermute | solution.py:27
  2.4 14.4 %collective-permute-start.1 = (bf16[480,128]{1,0:T(8,128)(2,1)S(1)}, bf16[480,128]{1,0:T(8,128)(2,1)S(1)}, u32[]{:S(2)}, u32[]{:S(2)}) collective-permute-start(bf16[480,128]{1,0:T(8,128)(2,1)S(1)} %get-tuple-element.20), channel_id=1, source_target_pairs={{1,2},{2,1},{3,4},{4,3},{5,6},{6,5},{7,8},{8,7},{9,10},{10,9},{11,... | collective-permute-start | bytes 368648 | tf_op jit(solution)/shard_map/ppermute | solution.py:27
  6.3 1.0 %copy-start = (bf16[64,61,25]{1,0,2:T(8,128)(2,1)S(1)}, bf16[64,61,25]{1,0,2:T(8,128)(2,1)}, u32[]{:S(2)}) copy-start(bf16[64,61,25]{1,0,2:T(8,128)(2,1)} %param.7) | copy-start | bytes 585604
  7.3 0.9 %copy-start.2 = (f32[25,8,128]{2,1,0:T(8,128)S(1)}, f32[25,8,128]{2,1,0:T(8,128)}, u32[]{:S(2)}) copy-start(f32[25,8,128]{2,1,0:T(8,128)} %param.6) | copy-start | bytes 307204
  17.3 7.6 %collective-permute-start.2 = (bf16[640,128]{1,0:T(8,128)(2,1)S(1)}, bf16[640,128]{1,0:T(8,128)(2,1)S(1)}, u32[]{:S(2)}, u32[]{:S(2)}) collective-permute-start(bf16[640,128]{1,0:T(8,128)(2,1)S(1)} %get-tuple-element.27), channel_id=1, source_target_pairs={{0,16},{16,0},{32,48},{48,32},{64,80},{80,64},{96,112},{112,96},{1... | collective-permute-start | bytes 491528 | tf_op jit(solution)/shard_map/ppermute | solution.py:27
  18.6 9.9 %collective-permute-start.3 = (bf16[640,128]{1,0:T(8,128)(2,1)S(1)}, bf16[640,128]{1,0:T(8,128)(2,1)S(1)}, u32[]{:S(2)}, u32[]{:S(2)}) collective-permute-start(bf16[640,128]{1,0:T(8,128)(2,1)S(1)} %get-tuple-element.28), channel_id=1, source_target_pairs={{16,32},{32,16},{48,64},{64,48},{80,96},{96,80},{112,128},{128,112... | collective-permute-start | bytes 491528 | tf_op jit(solution)/shard_map/ppermute | solution.py:27

commit v5 on v4

v5 whole, which is shorter than its diff:
```python
import jax
import jax.numpy as jnp
from jax import lax
from jax.experimental import pallas as pl
from jax.experimental.pallas import tpu as pltpu
from jax.sharding import PartitionSpec as P


F32 = jnp.float32
BF16 = jnp.bfloat16
SHIFT = 4


def vmem():
    return pl.BlockSpec(memory_space=pltpu.VMEM)


def params(mib):
    return pltpu.CompilerParams(vmem_limit_bytes=mib * 1024 * 1024)


def swap_pairs(array, axis, first):
    size = lax.axis_size(axis)
    pairs = []
    for low in range(first, size - 1, 2):
        pairs += [(low, low + 1), (low + 1, low)]
    return lax.ppermute(array, axis, pairs)


def is_upper():
    return lax.rem(lax.axis_index("rows"), 2) == 0


def open_kernel(raw_ref, far_ref, keep_ref):
    skip = raw_ref.shape[0] - far_ref.shape[0]
    even = lax.rem(lax.axis_index("tm"), 2) == 0
    start = pl.multiple_of(jnp.where(even, 0, skip), 16)
    far_ref[...] = raw_ref[pl.ds(start, far_ref.shape[0]), :].astype(BF16)
    keep_ref[...] = raw_ref[...]


def opening(raw, rows, taps):
    return pl.pallas_call(
        open_kernel,
        out_shape=(
            jax.ShapeDtypeStruct(((taps - 1) * rows, raw.shape[1]), BF16),
            jax.ShapeDtypeStruct(raw.shape, F32),
        ),
        in_specs=[vmem()],
        out_specs=(vmem(), vmem()),
        compiler_params=params(4),
        cost_estimate=pl.CostEstimate(flops=10**5, bytes_accessed=10**6, transcendentals=0),
        name="opening",
    )(raw)


def prep_kernel(
    line_ref, tmpl_ref, coef_in_ref, band_ref, sum_ref, even_ref, odd_ref, coef_ref, wide, mixed
):
    _, count, length = tmpl_ref.shape
    own_rows = coef_ref.shape[0]
    upper = is_upper()
    for a in range(5):
        source = jnp.where(upper, a, 4 - a) * (5 * own_rows)
        for r in range(own_rows):
            line = pl.ds(source + jnp.where(upper, r, own_rows - 1 - r), 5, stride=own_rows)
            coef_ref[r, 5 * a : 5 * a + 5, :] = coef_in_ref[line, :]
    rows = band_ref.shape[0]
    line = jnp.broadcast_to(line_ref[...], (rows, 256))
    band = pltpu.roll(line, 0, 1, stride=1, stride_axis=0)
    high = band.astype(BF16)
    low = (band - high.astype(F32)).astype(BF16)
    band_ref[:, 0:256] = high
    band_ref[:, 256:512] = low
    band_ref[:, 512:768] = high

    wide[...] = jnp.zeros_like(wide)
    for a in range(5):
        source = jnp.where(upper, a, 4 - a) * 5
        for b in range(5):
            wide[5 * a + b, :, 0:length] = tmpl_ref[source + b].astype(F32)

    def even_spot(k):
        return wide[10 * (k // 5) + k % 5]

    def odd_spot(k):
        return wide[10 * (k // 5) + 5 + k % 5]

    def both_spots(k):
        return even_spot(k) + odd_spot(k) if k < 10 else even_spot(k)

    slot = 0
    for out_ref, piece, size in ((sum_ref, both_spots, 15), (even_ref, even_spot, 15), (odd_ref, odd_spot, 10)):
        for p in range(0, size, 2):
            pair = piece(p)
            if p + 1 < size:
                pair = pair + pltpu.roll(piece(p + 1), 64, 1)
            for b in range(SHIFT):
                moved = pltpu.roll(pair, b, 1) if b else pair
                mixed[slot, pl.ds(b, count, stride=SHIFT), :] = moved
            out_ref[:, 64 * p : 64 * p + 128] = mixed[slot].astype(BF16)
            slot += 1


def prep(fir_taps, templates, coef, span, rows):
    count, _, spots = templates.shape
    taps = fir_taps.shape[0]
    line = jnp.pad(fir_taps[::-1], (span - taps + 1, 255 - span))[None]
    by_spot = jnp.transpose(templates, (2, 0, 1))
    return pl.pallas_call(
        prep_kernel,
        out_shape=(
            jax.ShapeDtypeStruct((2 * span, 768), BF16),
            jax.ShapeDtypeStruct((count * SHIFT, 16 * 64), BF16),
            jax.ShapeDtypeStruct((count * SHIFT, 16 * 64), BF16),
            jax.ShapeDtypeStruct((count * SHIFT, 10 * 64), BF16),
            jax.ShapeDtypeStruct((rows, 32, coef.shape[1]), F32),
        ),
        in_specs=[vmem()] * 3,
        out_specs=(vmem(),) * 5,
        scratch_shapes=[
            pltpu.VMEM((spots, count, 128), F32),
            pltpu.VMEM((21, count * SHIFT, 128), F32),
        ],
        compiler_params=params(8),
        cost_estimate=pl.CostEstimate(flops=10**7, bytes_accessed=2 * 10**6, transcendentals=0),
        name="prep",
    )(line, by_spot, coef)


def fir_kernel(band_ref, raw_ref, near_ref, far_ref, coef_ref, filt_ref, first_ref, second_ref, widened, block):
    rows, double, cols = filt_ref.shape
    span = double // 2
    half = rows // 2
    even = lax.rem(lax.axis_index("tm"), 2) == 0
    short = far_ref.shape[0]
    skip = widened.shape[0] - short
    widened[0:skip, :] = jnp.zeros((skip, cols), F32)
    widened[short:, :] = jnp.zeros((skip, cols), F32)
    widened[pl.ds(pl.multiple_of(jnp.where(even, skip, 0), 16), short), :] = far_ref[...].astype(F32)
    columns = []
    upper = is_upper()
    for r in range(rows):
        line = pl.ds(jnp.where(upper, r, rows - 1 - r), span, stride=rows)
        near = near_ref[line, :]
        far = widened[line, :]
        own = raw_ref[line, :]
        before = jnp.where(even, far, near)
        after = jnp.where(even, near, far)
        line = jnp.concatenate([before, own, after, jnp.zeros_like(own)], axis=0)
        high = line.astype(BF16)
        low = (line - high.astype(F32)).astype(BF16)
        columns.append(jnp.concatenate([high, high, low], axis=0))
    for r in range(0, rows, 2):
        pair = jnp.concatenate(columns[r : r + 2], axis=1)
        out = jnp.dot(band_ref[...], pair, preferred_element_type=F32).astype(BF16)
        filt_ref[r] = out[:, :cols]
        filt_ref[r + 1] = out[:, cols:]
    base = half * double
    for side, order, edge in (
        (first_ref, range(rows - 1, rows - half - 1, -1), (rows - 1, rows - 2)),
        (second_ref, range(half - 1, -1, -1), (1, 0)),
    ):
        for k, r in enumerate(order):
            side[double * k : double * (k + 1), :] = filt_ref[r]
        for k, r in enumerate(edge):
            block[...] = jnp.zeros_like(block)
            for a in range(5):
                block[5 * a : 5 * a + 5, :] = coef_ref[r, 20 - 5 * a : 25 - 5 * a, :]
            high = block[...].astype(BF16)
            side[base + 64 * k : base + 64 * k + 32, :] = high
            side[base + 64 * k + 32 : base + 64 * k + 64, :] = (block[...] - high.astype(F32)).astype(BF16)


def fir(band, raw, near, far, coef, rows):
    span = raw.shape[0] // rows
    cols = raw.shape[1]
    message = jax.ShapeDtypeStruct((rows // 2 * 2 * span + 128, cols), BF16)
    return pl.pallas_call(
        fir_kernel,
        out_shape=(jax.ShapeDtypeStruct((rows, 2 * span, cols), BF16), message, message),
        in_specs=[vmem()] * 5,
        out_specs=(vmem(),) * 3,
        scratch_shapes=[pltpu.VMEM(raw.shape, F32), pltpu.VMEM(coef.shape[1:], F32)],
        compiler_params=params(8),
        cost_estimate=pl.CostEstimate(flops=2 * 10**8, bytes_accessed=2 * 10**6, transcendentals=0),
        name="fir",
    )(band, raw, near, far, coef)


def shifter(shape):
    cols = shape[1]
    lane = lax.broadcasted_iota(jnp.int32, shape, 1)

    def shifted(x, b):
        if b == 2:
            return x
        out = pltpu.roll(x, (2 - b) % cols, 1)
        valid = lane >= 2 - b if b < 2 else lane < cols + 2 - b
        return jnp.where(valid, out, 0.0)

    return shifted


def closer(shape):
    span = shape[0] // 2
    last = lax.axis_index("tm") == lax.axis_size("tm") - 1
    time = lax.broadcasted_iota(jnp.int32, shape, 0)
    keep = jnp.logical_not(jnp.logical_and(last, time >= span))

    def closed(x):
        return jnp.where(keep, x, 0.0).astype(BF16).astype(F32)

    return closed


def build_slab(slab, x, shifted):
    double = x.shape[0]
    for b in range(5):
        moved = shifted(x, b)
        later = pltpu.roll(moved, double - SHIFT, 0)
        for f in range(4):
            piece = (later if f % 2 else moved)[8 * (f // 2) : 8 * (f // 2) + double - 16]
            slab[f, b] = piece.astype(BF16)


def inner_kernel(filt_ref, coef_ref, moved_ref, part_ref, white_ref, slab_ref):
    rows, double, cols = filt_ref.shape
    shifted = shifter((double, cols))
    closed = closer((double, cols))

    def spread(r, _):
        x = filt_ref[r].astype(F32)
        for b in range(5):
            moved_ref[b, r] = shifted(x, b)
        return 0

    lax.fori_loop(0, rows, spread, 0)

    def sums(r):
        total = jnp.zeros((double, cols), F32)
        for a in range(5):
            if 0 <= r + a - 2 < rows:
                for b in range(5):
                    s = 5 * a + b
                    total = total + coef_ref[r, s : s + 1, :] * moved_ref[b, r + a - 2]
        return total

    for k, r in enumerate((0, 1, rows - 2, rows - 1)):
        part_ref[k] = sums(r)
    for r in range(2, rows - 2):
        white_ref[r - 2] = closed(sums(r))
    build_slab(slab_ref.at[0], white_ref[1], shifted)
    build_slab(slab_ref.at[1], white_ref[3], shifted)
    build_slab(slab_ref.at[2], white_ref[0] - white_ref[1], shifted)
    build_slab(slab_ref.at[3], white_ref[2] - white_ref[3], shifted)
    build_slab(slab_ref.at[4], white_ref[2] - white_ref[1], shifted)


def inner(filt, coef):
    rows, double, cols = filt.shape
    return pl.pallas_call(
        inner_kernel,
        out_shape=(
            jax.ShapeDtypeStruct((5, rows, double, cols), F32),
            jax.ShapeDtypeStruct((4, double, cols), F32),
            jax.ShapeDtypeStruct((rows - 4, double, cols), F32),
            jax.ShapeDtypeStruct((5, 4, 5, double - 16, cols), BF16),
        ),
        in_specs=[vmem()] * 2,
        out_specs=(vmem(),) * 4,
        compiler_params=params(12),
        cost_estimate=pl.CostEstimate(flops=10**9, bytes_accessed=10**7, transcendentals=0),
        name="inner",
    )(filt, coef)


def spread_halo(side, halo, edge, shifted):
    half, double = halo.shape[1:3]

    def spread(k, _):
        x = side[pl.ds(pl.multiple_of(k * double, double), double), :].astype(F32)
        for b in range(5):
            halo[b, k] = shifted(x, b)
        return 0

    lax.fori_loop(0, half, spread, 0)
    base = half * double
    for k in range(2):
        high = side[base + 64 * k : base + 64 * k + 32, :].astype(F32)
        low = side[base + 64 * k + 32 : base + 64 * k + 64, :].astype(F32)
        edge[k] = high + low


def gather(total, weights, lines):
    for s, piece in lines:
        total = total + weights[s : s + 1, :] * piece
    return total


def after_kernel(side_ref, moved_ref, part_ref, mid_ref, coef_ref, white_ref, slab_ref, halo, edge, white):
    rows, double, cols = moved_ref.shape[1:]
    half = rows // 2
    shifted = shifter((double, cols))
    closed = closer((double, cols))
    spread_halo(side_ref, halo, edge, shifted)

    def lines(w, offsets):
        for a in offsets:
            row = w + a - half
            for b in range(5):
                yield 5 * a + b, moved_ref[b, row] if row < rows else halo[b, row - rows]

    zero = jnp.zeros((double, cols), F32)
    white[0] = closed(gather(part_ref[2], coef_ref.at[rows - 2], lines(rows, (4,))))
    white[1] = closed(gather(part_ref[3], coef_ref.at[rows - 1], lines(rows + 1, (3, 4))))
    white[2] = closed(gather(zero, edge.at[0], lines(rows + 2, range(5))))
    white[3] = closed(gather(zero, edge.at[1], lines(rows + 3, range(5))))
    white_ref[0] = white[0]
    white_ref[1] = white[1]
    build_slab(slab_ref.at[0], white[1], shifted)
    build_slab(slab_ref.at[1], white[3], shifted)
    build_slab(slab_ref.at[2], white[0] - white[1], shifted)
    build_slab(slab_ref.at[3], white[2] - white[3], shifted)
    build_slab(slab_ref.at[4], white[0] - mid_ref[rows - 5], shifted)
    build_slab(slab_ref.at[5], white[2] - white[1], shifted)


def after(side, inside, coef):
    moved, part, mid, _ = inside
    rows, double, cols = moved.shape[1:]
    return pl.pallas_call(
        after_kernel,
        out_shape=(
            jax.ShapeDtypeStruct((2, double, cols), F32),
            jax.ShapeDtypeStruct((6, 4, 5, double - 16, cols), BF16),
        ),
        in_specs=[vmem()] * 5,
        out_specs=(vmem(),) * 2,
        scratch_shapes=[
            pltpu.VMEM((5, rows // 2, double, cols), F32),
            pltpu.VMEM((2, 32, cols), F32),
            pltpu.VMEM((4, double, cols), F32),
        ],
        compiler_params=params(12),
        cost_estimate=pl.CostEstimate(flops=10**9, bytes_accessed=10**7, transcendentals=0),
        name="after",
    )(side, moved, part, mid, coef)


def match_kernel(
    side_ref,
    moved_ref,
    part_ref,
    mid_ref,
    mid_slab_ref,
    low_ref,
    low_slab_ref,
    coef_ref,
    sum_ref,
    even_ref,
    odd_ref,
    white_hbm,
    best_hbm,
    halo,
    edge,
    white,
    slabs,
    natural,
    rounded,
    best,
    sems,
):
    rows, double, cols = moved_ref.shape[1:]
    span = double // 2
    half = rows // 2
    shifted = shifter((double, cols))
    closed = closer((double, cols))
    upper = is_upper()

    def actual(r):
        return jnp.where(upper, r, rows - 1 - r)

    spread_halo(side_ref, halo, edge, shifted)

    def lines(w, offsets):
        for a in offsets:
            row = w + a
            for b in range(5):
                yield 5 * a + b, halo[b, row] if row < half else moved_ref[b, row - half]

    zero = jnp.zeros((double, cols), F32)
    white[0] = closed(gather(zero, edge.at[0], lines(0, range(5))))
    white[1] = closed(gather(zero, edge.at[1], lines(1, range(5))))
    white[2] = closed(gather(part_ref[0], coef_ref.at[0], lines(2, (0, 1))))
    white[3] = closed(gather(part_ref[1], coef_ref.at[1], lines(3, (0,))))
    for r in range(rows):
        if r < 2:
            line = white[r + 2, 0:span]
        elif r < rows - 2:
            line = mid_ref[r - 2, 0:span]
        else:
            line = low_ref[r - rows + 2, 0:span]
        natural[pl.ds(actual(r), span, stride=rows), :] = line
    rounded[...] = natural[...].astype(BF16)
    white_copy = pltpu.make_async_copy(rounded, white_hbm, sems.at[span // (4 * SHIFT)])
    white_copy.start()

    build_slab(slabs.at[0], white[1], shifted)
    build_slab(slabs.at[1], white[3], shifted)
    build_slab(slabs.at[2], white[0] - white[1], shifted)
    build_slab(slabs.at[3], white[2] - white[3], shifted)
    build_slab(slabs.at[4], white[2] - white[1], shifted)
    build_slab(slabs.at[5], mid_ref[0] - white[3], shifted)
    high = [slabs.at[k] for k in range(6)]
    mid = [mid_slab_ref.at[k] for k in range(5)]
    low = [low_slab_ref.at[k] for k in range(6)]
    plain = high[0:2] + mid[0:2] + low[0:2]
    level = high[2:4] + mid[2:4] + low[2:4]
    step = high[4:6] + mid[4:5] + low[4:6]

    def product(lhs_ref, source, f, start, depth):
        blank = [jnp.zeros((64, cols), BF16)] * (depth % 2)
        columns = [
            jnp.concatenate(
                [source[m + j][f, b, pl.ds(start, 64), :] for j in range(depth) for b in range(5)] + blank, axis=0
            )
            for m in range(half)
        ]
        found = jnp.dot(lhs_ref[...], jnp.concatenate(columns, axis=1), preferred_element_type=F32)
        return found.reshape(found.shape[0] // 8, 8, half * cols)

    def top(found):
        high = jnp.max(found, axis=0)
        return jnp.maximum(high, pltpu.roll(high, 4, 0))

    chunk = 4 * SHIFT * rows

    def sent(q):
        part = pl.ds(pl.multiple_of(q * chunk, chunk), chunk)
        return pltpu.make_async_copy(best.at[part, :], best_hbm.at[part, :], sems.at[q])

    def score(q, _):
        start = pl.multiple_of(q * 16, 16)
        for f in range(4):
            shared = product(sum_ref, plain, f, start, 3)
            found = (
                top(product(even_ref, level, f, start, 3) + shared),
                top(product(odd_ref, step, f, start, 2) + shared),
            )
            for r in range(rows):
                first_row = q * chunk + SHIFT * rows * f + actual(r)
                m = r // 2
                best[pl.ds(first_row, SHIFT, stride=rows), :] = found[r % 2][0:SHIFT, cols * m : cols * (m + 1)]
        sent(q).start()
        return 0

    parts = span // (4 * SHIFT)
    lax.fori_loop(0, parts, score, 0)
    for q in range(parts):
        sent(q).wait()
    white_copy.wait()


def match(inside, lower, second, coef, bands):
    moved, part, mid, mid_slabs = inside
    rows, double, cols = moved.shape[1:]
    span = double // 2
    return pl.pallas_call(
        match_kernel,
        out_shape=(
            jax.ShapeDtypeStruct((span * rows, cols), BF16),
            jax.ShapeDtypeStruct((span * rows, cols), F32),
        ),
        in_specs=[vmem()] * 11,
        out_specs=(pl.BlockSpec(memory_space=pltpu.HBM),) * 2,
        scratch_shapes=[
            pltpu.VMEM((5, rows // 2, double, cols), F32),
            pltpu.VMEM((2, 32, cols), F32),
            pltpu.VMEM((4, double, cols), F32),
            pltpu.VMEM((6, 4, 5, double - 16, cols), BF16),
            pltpu.VMEM((span * rows, cols), F32),
            pltpu.VMEM((span * rows, cols), BF16),
            pltpu.VMEM((span * rows, cols), F32),
            pltpu.SemaphoreType.DMA((span // (4 * SHIFT) + 1,)),
        ],
        compiler_params=params(16),
        cost_estimate=pl.CostEstimate(flops=11 * 10**9, bytes_accessed=10**7, transcendentals=0),
        name="match",
    )(second, moved, part, mid, mid_slabs, *lower, coef, *bands)


def shards(raw_signal, fir_taps, white_coef, templates):
    span, rows, cols = raw_signal.shape
    raw = raw_signal.reshape(span * rows, cols)
    coef = white_coef.reshape(-1, cols)
    far, raw = opening(raw, rows, fir_taps.shape[0])
    far = swap_pairs(far, "tm", 1)
    near = swap_pairs(raw, "tm", 0)
    band, *bands, coef = prep(fir_taps, templates, coef, span, rows)
    filt, first, second = fir(band, raw, near, far, coef, rows)
    first = swap_pairs(first, "rows", 0)
    second = swap_pairs(second, "rows", 1)
    inside = inner(filt, coef)
    lower = after(first, inside, coef)
    whitened, best = match(inside, lower, second, coef, bands)
    return whitened.reshape(span, rows, cols), best.reshape(span, rows, cols)


def solution(mesh):
    return jax.shard_map(
        shards,
        mesh=mesh,
        in_specs=(P("tm", "rows", None), P(), P(None, "rows", None), P()),
        out_specs=(P("tm", "rows", None), P("tm", "rows", None)),
        check_vma=False,
    )
```

time: 45.2 us -> 43.6 us (0.965)
  waiting for transfers between devices: 10.1 us -> 9.26 us
  Pallas kernels: 21.1 us -> 20.5 us
    pallas_call x1, Pallas kernels: 16.4 us -> 14.7 us  [match(): pl.pallas_call(match_kernel, out_shape=(jax.ShapeDtypeStruct((span * rows...]
    pallas_call x0 -> x1, Pallas kernels: none -> 1.1 us  [after(): pl.pallas_call(after_kernel, out_shape=(jax.ShapeDtypeStruct((2, double,...]
    ppermute x4, waiting for transfers between devices: 10.1 us -> 9.26 us  [swap_pairs(): return lax.ppermute(array, axis, pairs)]
  transfers between devices with their start and end apart: 4 -> 4, of which waited for: 2 -> 2; matrix products, arithmetic and copies ran while one was open for 2% -> 2% of each run, Pallas kernels for 9% -> 12%
where the time goes in v5:
time: 43.6 us; the launch traced here: 43.4 us
  Pallas kernels  20.5 us (47%)
  starting transfers between devices  9.3 us (21%)
  waiting for transfers between devices  9.26 us (21%)
  local copies, waits for them, and re-layouts  3.66 us (8%)
  between operations  0.7 us (2%)
    pallas_call x1, Pallas kernels, match(): pl.pallas_call(match_kernel, out_shape=(jax.ShapeDtypeStruct((span * rows...  14.7 us
    ppermute x4, starting transfers between devices, swap_pairs(): return lax.ppermute(array, axis, pairs)  9.3 us
    ppermute x4, waiting for transfers between devices, swap_pairs(): return lax.ppermute(array, axis, pairs)  9.26 us
    unnamed x6, local copies, waits for them, and re-layouts  2.84 us
    pallas_call x1, Pallas kernels, prep(): pl.pallas_call(prep_kernel, out_shape=(jax.ShapeDtypeStruct((2 * span, 76...  2.05 us
    pallas_call x1, Pallas kernels, inner(): pl.pallas_call(inner_kernel, out_shape=(jax.ShapeDtypeStruct((5, rows, do...  1.91 us
    pallas_call x1, Pallas kernels, after(): pl.pallas_call(after_kernel, out_shape=(jax.ShapeDtypeStruct((2, double,...  1.1 us
  transfers between devices with their start and end apart: 4, of which 2 were waited for; matrix products, arithmetic and copies ran while one was open for 2% of the time, Pallas kernels for 12%

profile of v5, /device:TPU:201, one launch (start us, length us, event | category | flops | bytes accessed | tf_op | source)
XLA Modules:
  0.0 43.4 jit_solution(18153410336529950514)
XLA Ops:
  0.6 0.0 copy-start.1
  0.6 0.9 %copy-done.1 = f32[64,8,128]{2,1,0:T(8,128)S(1)} copy-done((f32[64,8,128]{2,1,0:T(8,128)S(1)}, f32[64,8,128]{2,1,0:T(8,128)}, u32[]{:S(2)}) %copy-start.1) | copy-done | bytes 262168
  1.6 0.8 %collective-permute-start = (f32[512,128]{1,0:T(8,128)S(1)}, f32[512,128]{1,0:T(8,128)S(1)}, u32[]{:S(2)}, u32[]{:S(2)}) collective-permute-start(f32[512,128]{1,0:T(8,128)S(1)} %get-tuple-element.21.raw_ref), channel_id=1, source_target_pairs={{0,1},{1,0},{2,3},{3,2},{4,5},{5,4},{6,7},{7,6},{8,9},{9,8},{10,11... | collective-permute-start | bytes 786440 | tf_op jit(solution)/shard_map/ppermute | solution.py:27
  2.4 3.1 %collective-permute-start.1 = (bf16[480,128]{1,0:T(8,128)(2,1)S(1)}, bf16[480,128]{1,0:T(8,128)(2,1)S(1)}, u32[]{:S(2)}, u32[]{:S(2)}) collective-permute-start(bf16[480,128]{1,0:T(8,128)(2,1)S(1)} %get-tuple-element.22), channel_id=1, source_target_pairs={{1,2},{2,1},{3,4},{4,3},{5,6},{6,5},{7,8},{8,7},{9,10},{10,9},{11,... | collective-permute-start | bytes 368648 | tf_op jit(solution)/shard_map/ppermute | solution.py:27
  5.5 0.7 %rev.3 = f32[61]{0:T(128)S(1)} reverse(f32[61]{0:T(128)} %param.5), dimensions={0} | reverse | bytes 488 | tf_op jit(solution)/shard_map/rev | solution.py:108
  6.2 0.1 pad.4
  6.3 0.0 copy-start
  6.3 1.0 %copy-done = bf16[64,61,25]{1,0,2:T(8,128)(2,1)S(1)} copy-done((bf16[64,61,25]{1,0,2:T(8,128)(2,1)S(1)}, bf16[64,61,25]{1,0,2:T(8,128)(2,1)}, u32[]{:S(2)}) %copy-start) | copy-done | bytes 195224
  7.3 0.0 copy-start.2
  7.3 0.9 %copy-done.2 = f32[25,8,128]{2,1,0:T(8,128)S(1)} copy-done((f32[25,8,128]{2,1,0:T(8,128)S(1)}, f32[25,8,128]{2,1,0:T(8,128)}, u32[]{:S(2)}) %copy-start.2) | copy-done | bytes 102424
  8.2 2.0 %prep.1 = (bf16[128,768]{1,0:T(8,128)(2,1)S(1)}, bf16[256,1024]{1,0:T(8,128)(2,1)S(1)}, bf16[256,1024]{1,0:T(8,128)(2,1)S(1)}, bf16[256,640]{1,0:T(8,128)(2,1)S(1)}, f32[8,32,128]{2,1,0:T(8,128)S(1)}) custom-call(f32[1,256]{1,0:T(1,128)S(1)} %bitcast.9, bf16[25,64,61]{2,1,0:T(8,128)(2,1)S(1)} %bitcast.6, f32[200,128]{1,0:T(8,128)S(1)} %bitcast.8), custom_call_target="tpu_custom_call" | custom-call | flops 10000000 | bytes 2000000 | tf_op jit(solution)/shard_map/prep/pallas_call | solution.py:110
  10.2 6.5 %collective-permute-done.1.far_ref = bf16[480,128]{1,0:T(8,128)(2,1)S(1)} collective-permute-done((bf16[480,128]{1,0:T(8,128)(2,1)S(1)}, bf16[480,128]{1,0:T(8,128)(2,1)S(1)}, u32[]{:S(2)}, u32[]{:S(2)}) %collective-permute-start.1) | collective-permute-done | bytes 122912 | tf_op jit(solution)/shard_map/ppermute | solution.py:27
  16.8 0.0 collective-permute-done.near_ref
  16.8 0.6 %fir.1 = (bf16[8,128,128]{2,1,0:T(8,128)(2,1)S(1)}, bf16[640,128]{1,0:T(8,128)(2,1)S(1)}, bf16[640,128]{1,0:T(8,128)(2,1)S(1)}) custom-call(bf16[128,768]{1,0:T(8,128)(2,1)S(1)} %get-tuple-element.20.band_ref, f32[512,128]{1,0:T(8,128)S(1)} %get-tuple-element.21.raw_ref, f32[512,128]{1,0:T(8,128)S(1)} %collective-permute-done.near_ref, ...), custom_call_target="tpu_custom_call" | custom-call | flops 200000000 | bytes 2000000 | tf_op jit(solution)/shard_map/fir/pallas_call | solution.py:179
  17.4 1.3 %collective-permute-start.3 = (bf16[640,128]{1,0:T(8,128)(2,1)S(1)}, bf16[640,128]{1,0:T(8,128)(2,1)S(1)}, u32[]{:S(2)}, u32[]{:S(2)}) collective-permute-start(bf16[640,128]{1,0:T(8,128)(2,1)S(1)} %get-tuple-element.30), channel_id=1, source_target_pairs={{0,16},{16,0},{32,48},{48,32},{64,80},{80,64},{96,112},{112,96},{1... | collective-permute-start | bytes 491528 | tf_op jit(solution)/shard_map/ppermute | solution.py:27
  18.7 4.2 %collective-permute-start.2 = (bf16[640,128]{1,0:T(8,128)(2,1)S(1)}, bf16[640,128]{1,0:T(8,128)(2,1)S(1)}, u32[]{:S(2)}, u32[]{:S(2)}) collective-permute-start(bf16[640,128]{1,0:T(8,128)(2,1)S(1)} %get-tuple-element.24), channel_id=1, source_target_pairs={{16,32},{32,16},{48,64},{64,48},{80,96},{96,80},{112,128},{128,112... | collective-permute-start | bytes 491528 | tf_op jit(solution)/shard_map/ppermute | solution.py:27
  22.9 1.9 %inner.1 = (f32[5,8,128,128]{3,2,1,0:T(8,128)S(1)}, f32[4,128,128]{2,1,0:T(8,128)S(1)}, f32[4,128,128]{2,1,0:T(8,128)S(1)}, bf16[5,4,5,112,128]{4,3,2,1,0:T(8,128)(2,1)S(1)}) custom-call(bf16[8,128,128]{2,1,0:T(8,128)(2,1)S(1)} %get-tuple-element.25.filt_ref, f32[8,32,128]{2,1,0:T(8,128)S(1)} %get-tuple-element.23.coef_ref), custom_call_target="tpu_custom_call" | custom-call | flops 1000000000 | bytes 10000000 | tf_op jit(solution)/shard_map/inner/pallas_call | solution.py:262
  24.8 0.0 collective-permute-done.3.side_ref
  24.8 1.1 %after.1 = (f32[2,128,128]{2,1,0:T(8,128)S(1)}, bf16[6,4,5,112,128]{4,3,2,1,0:T(8,128)(2,1)S(1)}) custom-call(bf16[640,128]{1,0:T(8,128)(2,1)S(1)} %collective-permute-done.3.side_ref, f32[5,8,128,128]{3,2,1,0:T(8,128)S(1)} %get-tuple-element.26.moved_ref, f32[4,128,128]{2,1,0:T(8,128)S(1)} %get-tuple-element.27.part_ref, ...), custom_call_target="tpu_custom_call" | custom-call | flops 1000000000 | bytes 10000000 | tf_op jit(solution)/shard_map/after/pallas_call | solution.py:332
  25.9 2.7 %collective-permute-done.2.side_ref = bf16[640,128]{1,0:T(8,128)(2,1)S(1)} collective-permute-done((bf16[640,128]{1,0:T(8,128)(2,1)S(1)}, bf16[640,128]{1,0:T(8,128)(2,1)S(1)}, u32[]{:S(2)}, u32[]{:S(2)}) %collective-permute-start.2) | collective-permute-done | bytes 163872 | tf_op jit(solution)/shard_map/ppermute | solution.py:27
  28.6 14.7 %match.1 = (bf16[512,128]{1,0:T(8,128)(2,1)}, f32[512,128]{1,0:T(8,128)}) custom-call(bf16[640,128]{1,0:T(8,128)(2,1)S(1)} %collective-permute-done.2.side_ref, f32[5,8,128,128]{3,2,1,0:T(8,128)S(1)} %get-tuple-element.26.moved_ref, f32[4,128,128]{2,1,0:T(8,128)S(1)} %get-tuple-element.27.part_ref, f32[4,128,128]{2,1,0:T(8,128)S(1)} %get-tuple-element.28.mid_ref, ...), custom_call_target="tpu_custom_call" | custom-call | flops 11000000512 | bytes 10000000 | tf_op jit(solution)/shard_map/match/pallas_call | solution.py:469
  (1 shorter events, 0.0 us)
Async XLA Ops:
  0.6 1.0 %copy-start.1 = (f32[64,8,128]{2,1,0:T(8,128)S(1)}, f32[64,8,128]{2,1,0:T(8,128)}, u32[]{:S(2)}) copy-start(f32[64,8,128]{2,1,0:T(8,128)} %param.4) | copy-start | bytes 786436
  1.6 15.2 %collective-permute-start = (f32[512,128]{1,0:T(8,128)S(1)}, f32[512,128]{1,0:T(8,128)S(1)}, u32[]{:S(2)}, u32[]{:S(2)}) collective-permute-start(f32[512,128]{1,0:T(8,128)S(1)} %get-tuple-element.21.raw_ref), channel_id=1, source_target_pairs={{0,1},{1,0},{2,3},{3,2},{4,5},{5,4},{6,7},{7,6},{8,9},{9,8},{10,11... | collective-permute-start | bytes 786440 | tf_op jit(solution)/shard_map/ppermute | solution.py:27
  2.4 14.4 %collective-permute-start.1 = (bf16[480,128]{1,0:T(8,128)(2,1)S(1)}, bf16[480,128]{1,0:T(8,128)(2,1)S(1)}, u32[]{:S(2)}, u32[]{:S(2)}) collective-permute-start(bf16[480,128]{1,0:T(8,128)(2,1)S(1)} %get-tuple-element.22), channel_id=1, source_target_pairs={{1,2},{2,1},{3,4},{4,3},{5,6},{6,5},{7,8},{8,7},{9,10},{10,9},{11,... | collective-permute-start | bytes 368648 | tf_op jit(solution)/shard_map/ppermute | solution.py:27
  6.3 1.0 %copy-start = (bf16[64,61,25]{1,0,2:T(8,128)(2,1)S(1)}, bf16[64,61,25]{1,0,2:T(8,128)(2,1)}, u32[]{:S(2)}) copy-start(bf16[64,61,25]{1,0,2:T(8,128)(2,1)} %param.7) | copy-start | bytes 585604
  7.3 0.9 %copy-start.2 = (f32[25,8,128]{2,1,0:T(8,128)S(1)}, f32[25,8,128]{2,1,0:T(8,128)}, u32[]{:S(2)}) copy-start(f32[25,8,128]{2,1,0:T(8,128)} %param.6) | copy-start | bytes 307204
  17.4 7.4 %collective-permute-start.3 = (bf16[640,128]{1,0:T(8,128)(2,1)S(1)}, bf16[640,128]{1,0:T(8,128)(2,1)S(1)}, u32[]{:S(2)}, u32[]{:S(2)}) collective-permute-start(bf16[640,128]{1,0:T(8,128)(2,1)S(1)} %get-tuple-element.30), channel_id=1, source_target_pairs={{0,16},{16,0},{32,48},{48,32},{64,80},{80,64},{96,112},{112,96},{1... | collective-permute-start | bytes 491528 | tf_op jit(solution)/shard_map/ppermute | solution.py:27
  18.7 9.9 %collective-permute-start.2 = (bf16[640,128]{1,0:T(8,128)(2,1)S(1)}, bf16[640,128]{1,0:T(8,128)(2,1)S(1)}, u32[]{:S(2)}, u32[]{:S(2)}) collective-permute-start(bf16[640,128]{1,0:T(8,128)(2,1)S(1)} %get-tuple-element.24), channel_id=1, source_target_pairs={{16,32},{32,16},{48,64},{64,48},{80,96},{96,80},{112,128},{128,112... | collective-permute-start | bytes 491528 | tf_op jit(solution)/shard_map/ppermute | solution.py:27
